TPU v7x, 32 devices: a whole 2x2x4 slice. The times are simulated.
32 devices in a mesh: dp: 16 (over z, x, core), tensor: 2 (over y).
Axes of the slice: x: 2, y: 2, z: 4, core: 2. Of those that a mesh axis runs over, the one named last changes fastest.
Arguments:
- tokens: bfloat16 [16, 1024, 1536], P('dp', 'tensor'), may hold values from -6 to 6
- segment_ids: int32 [16, 1024], P('dp'), may hold values from 0 to 5, as said below
- positions: int32 [16, 1024], P('dp'), may hold values from 0 to 1023, as said below
- query_weight: float32 [1536, 1536], P('dp', 'tensor'), may hold values from -0.15625 to 0.15625
- key_master_weight: float32 [1536, 768], P('dp', 'tensor'), may hold values from -0.15625 to 0.15625
- value_master_weight: float32 [1536, 768], P('dp', 'tensor'), may hold values from -0.15625 to 0.15625
- out_weight: float32 [1536, 1536], P('tensor', 'dp'), may hold values from -1.25 to 1.25
- attn_gain: float32 [1536], P('dp'), may hold values from 0.5 to 1.5
- gate_weight: float32 [1536, 4096], P('dp', 'tensor'), may hold values from -0.15625 to 0.15625
- up_weight: float32 [1536, 4096], P('dp', 'tensor'), may hold values from -0.15625 to 0.15625
- down_weight: float32 [4096, 1536], P('tensor', 'dp'), may hold values from -0.09375 to 0.09375
- mlp_gain: float32 [1536], P('dp'), may hold values from 0.5 to 1.5
- cotangent: bfloat16 [16, 1024, 1536], P('dp', 'tensor'), may hold values from -8 to 8
Outputs:
- output: bfloat16 [16, 1024, 1536], P('dp', 'tensor')
- input_grad: bfloat16 [16, 1024, 1536], P('dp', 'tensor')
- grad_query_weight: float32 [1536, 1536], P('dp', 'tensor')
- grad_key_weight: float32 [1536, 768], P('dp', 'tensor')
- grad_value_weight: float32 [1536, 768], P('dp', 'tensor')
- grad_out_weight: float32 [1536, 1536], P('tensor', 'dp')
- grad_attn_gain: float32 [1536], P('dp')
- grad_gate_weight: float32 [1536, 4096], P('dp', 'tensor')
- grad_up_weight: float32 [1536, 4096], P('dp', 'tensor')
- grad_down_weight: float32 [4096, 1536], P('tensor', 'dp')
- grad_mlp_gain: float32 [1536], P('dp')
Inputs may be any that keep to these rules, and one draw needn't show every extreme that they name: `segment_ids`: along each sequence the ids start at 0 and rise by one at the first token of each document; every document except a sequence's last holds at least 204 tokens. `positions`: each token's place within its document: 0 at a document's first token, rising by one along it.
All inputs are finite; a program needn't handle non-finite values.
Results may differ from a plain program's by a relative error of at most 0.018.
Values may be sent and summed in bfloat16 or wider, within the bound.
No kernel may reach another device: no remote copies, remote signals or barrier semaphores. Data moves between devices by JAX's collectives and lax.ppermute only.
A program may use at most 192 MiB of HBM per device.

v0:
```python
import math

import jax
import jax.numpy as jnp
from jax import lax
from jax.sharding import PartitionSpec as P

HEAD_DIM = 96


EPSILON = 1e-05
ROPE_BASE = 100000.0
MASKED = -1000000000.0
BLOCK_ROWS = 512


def rope_tables(places, head_width):
    half_width = head_width // 2
    ladder = jnp.arange(half_width, dtype=jnp.float32)
    inverse = jnp.power(jnp.float32(ROPE_BASE), -2.0 * ladder / head_width)
    angles = places.astype(jnp.float32)[..., None] * inverse
    cosine_table = jnp.cos(angles)
    sine_table = jnp.sin(angles)
    return (
        jnp.concatenate([cosine_table, cosine_table], -1),
        jnp.concatenate([sine_table, sine_table], -1),
    )


def rotate_pairs(value_tensor):
    half_width = value_tensor.shape[-1] // 2
    return jnp.concatenate([-value_tensor[..., half_width:], value_tensor[..., :half_width]], -1)


def unrotate(value_tensor):
    half_width = value_tensor.shape[-1] // 2
    return jnp.concatenate([value_tensor[..., half_width:], -value_tensor[..., :half_width]], -1)


def apply_rope(value_tensor, cosine_table, sine_table):
    return value_tensor * cosine_table + rotate_pairs(value_tensor) * sine_table


def rope_back(grads_in, cosine_table, sine_table):
    return grads_in * cosine_table + unrotate(grads_in * sine_table)


def rms_inverse(value_tensor):
    return lax.rsqrt(jnp.mean(value_tensor * value_tensor, -1, keepdims=True) + EPSILON)


def norm_back(upstream, value_tensor, inverse, gain_vec):
    scaled = upstream * gain_vec
    inner_mean = jnp.mean(scaled * value_tensor, -1, keepdims=True)
    passed_back = inverse * (scaled - value_tensor * inverse * inverse * inner_mean)
    gain_grad = jnp.sum(upstream * value_tensor * inverse, axis=(0, 1))
    return (passed_back, gain_grad)


def split_groups(value_tensor, seq_count, groups):
    row_count, item_width = value_tensor.shape
    token_length = row_count // seq_count
    grouped = value_tensor.reshape(seq_count, token_length, groups, item_width // groups)
    return grouped.transpose(0, 2, 1, 3).reshape(
        seq_count * groups, token_length, item_width // groups
    )


def join_groups(value_tensor, seq_count):
    item_count, token_length, item_width = value_tensor.shape
    groups = item_count // seq_count
    grouped = value_tensor.reshape(seq_count, groups, token_length, item_width)
    return grouped.transpose(0, 2, 1, 3).reshape(seq_count * token_length, groups * item_width)


def block_mask(segments, offset, block_len):
    token_length = segments.shape[0]
    row_segs = lax.dynamic_slice_in_dim(segments, offset, block_len, 0)
    row_place = offset + jnp.arange(block_len)
    col_place = jnp.arange(token_length)
    return (row_segs[:, None] == segments[None, :]) & (row_place[:, None] >= col_place[None, :])


def attend_forward(entries):
    query_tensor, key_tensor, value_tensor, segments = entries
    token_length = key_tensor.shape[0]
    block_len = min(BLOCK_ROWS, token_length)
    block_count = token_length // block_len
    score_scale = 1.0 / math.sqrt(key_tensor.shape[-1])

    def one_block(number):
        offset = number * block_len
        query_block = lax.dynamic_slice_in_dim(query_tensor, offset, block_len, 0)
        allowed = block_mask(segments, offset, block_len)
        scores = (
            jnp.einsum("qrd,kd->rqk", query_block, key_tensor, preferred_element_type=jnp.float32)
            * score_scale
        )
        scores = jnp.where(allowed[None], scores, MASKED)
        highest = jnp.max(scores, -1, keepdims=True)
        expo_scores = jnp.exp(scores - highest)
        totals = jnp.sum(expo_scores, -1, keepdims=True)
        probabilities = (expo_scores / totals).astype(jnp.bfloat16)
        outcome = jnp.einsum(
            "rqk,kd->qrd", probabilities, value_tensor, preferred_element_type=jnp.float32
        ).astype(jnp.bfloat16)
        return (outcome, (highest + jnp.log(totals))[..., 0])

    outcomes, log_totals = lax.map(one_block, jnp.arange(block_count))
    return (outcomes.reshape(query_tensor.shape), log_totals)


def attend_backward(entries):
    query_tensor, key_tensor, value_tensor, grads_out, log_totals, segments = entries
    token_length = key_tensor.shape[0]
    block_len = min(BLOCK_ROWS, token_length)
    block_count = token_length // block_len
    score_scale = 1.0 / math.sqrt(key_tensor.shape[-1])

    def one_block(carried, inputs):
        key_grad, value_grad = carried
        number, block_totals = inputs
        offset = number * block_len
        query_block = lax.dynamic_slice_in_dim(query_tensor, offset, block_len, 0)
        grad_block = lax.dynamic_slice_in_dim(grads_out, offset, block_len, 0)
        allowed = block_mask(segments, offset, block_len)
        scores = (
            jnp.einsum("qrd,kd->rqk", query_block, key_tensor, preferred_element_type=jnp.float32)
            * score_scale
        )
        scores = jnp.where(allowed[None], scores, MASKED)
        probabilities = jnp.exp(scores - block_totals[..., None])
        prob_grads = jnp.einsum(
            "qrd,kd->rqk", grad_block, value_tensor, preferred_element_type=jnp.float32
        )
        row_terms = jnp.sum(probabilities * prob_grads, -1, keepdims=True)
        score_grads = (probabilities * (prob_grads - row_terms)).astype(jnp.bfloat16)
        query_grad = (
            jnp.einsum("rqk,kd->qrd", score_grads, key_tensor, preferred_element_type=jnp.float32)
            * score_scale
        )
        key_grad = (
            key_grad
            + jnp.einsum(
                "rqk,qrd->kd", score_grads, query_block, preferred_element_type=jnp.float32
            )
            * score_scale
        )
        value_grad = value_grad + jnp.einsum(
            "rqk,qrd->kd",
            probabilities.astype(jnp.bfloat16),
            grad_block,
            preferred_element_type=jnp.float32,
        )
        return ((key_grad, value_grad), query_grad)

    zeros_kv = jnp.zeros(key_tensor.shape, jnp.float32)
    sums_kv, query_grads = lax.scan(
        one_block, (zeros_kv, zeros_kv), (jnp.arange(block_count), log_totals)
    )
    return (query_grads.reshape(query_tensor.shape), sums_kv[0], sums_kv[1])


def body(
    tokens,
    segment_ids,
    positions,
    query_weight,
    key_master_weight,
    value_master_weight,
    out_weight,
    attn_gain,
    gate_weight,
    up_weight,
    down_weight,
    mlp_gain,
    cotangent,
):
    seq_count, half_rows, model_width = tokens.shape
    token_length = segment_ids.shape[1]
    row_count = seq_count * token_length
    full_query, full_key, full_value, full_out, attn_scale = (
        lax.all_gather(query_weight.astype(jnp.bfloat16), "dp", axis=0, tiled=True),
        lax.all_gather(key_master_weight.astype(jnp.bfloat16), "dp", axis=0, tiled=True),
        lax.all_gather(value_master_weight.astype(jnp.bfloat16), "dp", axis=0, tiled=True),
        lax.all_gather(out_weight.astype(jnp.bfloat16), "dp", axis=1, tiled=True),
        lax.all_gather(attn_gain.astype(jnp.bfloat16), "dp", axis=0, tiled=True),
    )
    head_width = HEAD_DIM
    local_heads = full_query.shape[1] // head_width
    local_groups = full_key.shape[1] // head_width
    group_ratio = local_heads // local_groups
    item_count = seq_count * local_groups
    cosine_table, sine_table = rope_tables(positions, head_width)
    cosine_table = cosine_table.reshape(row_count, 1, head_width)
    sine_table = sine_table.reshape(row_count, 1, head_width)
    residual = tokens.astype(jnp.float32)
    inverse_one = rms_inverse(residual)
    gain_one = attn_scale.astype(jnp.float32)
    normed_one = (residual * inverse_one * gain_one).astype(jnp.bfloat16)
    rows_one = lax.all_gather(normed_one, "tensor", axis=1, tiled=True).reshape(
        row_count, model_width
    )
    query_raw = jnp.dot(rows_one, full_query, preferred_element_type=jnp.float32).reshape(
        row_count, local_heads, head_width
    )
    key_raw = jnp.dot(rows_one, full_key, preferred_element_type=jnp.float32).reshape(
        row_count, local_groups, head_width
    )
    value_rows = jnp.dot(rows_one, full_value, preferred_element_type=jnp.float32).astype(
        jnp.bfloat16
    )
    query_rows = (
        apply_rope(query_raw, cosine_table, sine_table)
        .astype(jnp.bfloat16)
        .reshape(row_count, local_heads * head_width)
    )
    key_rows = (
        apply_rope(key_raw, cosine_table, sine_table)
        .astype(jnp.bfloat16)
        .reshape(row_count, local_groups * head_width)
    )
    query_items = split_groups(query_rows, seq_count, local_groups).reshape(
        item_count, token_length, group_ratio, head_width
    )
    key_items = split_groups(key_rows, seq_count, local_groups)
    value_items = split_groups(value_rows, seq_count, local_groups)
    segment_items = jnp.repeat(segment_ids, local_groups, axis=0)
    attended_items, log_totals = lax.map(
        attend_forward, (query_items, key_items, value_items, segment_items)
    )
    attended = join_groups(
        attended_items.reshape(item_count, token_length, group_ratio * head_width), seq_count
    )
    attn_partial = jnp.dot(attended, full_out, preferred_element_type=jnp.float32).reshape(
        seq_count, token_length, model_width
    )
    middle = residual + lax.psum_scatter(
        attn_partial.astype(jnp.bfloat16), "tensor", scatter_dimension=1, tiled=True
    ).astype(jnp.float32)
    full_gate, full_up, full_down, mlp_scale = (
        lax.all_gather(gate_weight.astype(jnp.bfloat16), "dp", axis=0, tiled=True),
        lax.all_gather(up_weight.astype(jnp.bfloat16), "dp", axis=0, tiled=True),
        lax.all_gather(down_weight.astype(jnp.bfloat16), "dp", axis=1, tiled=True),
        lax.all_gather(mlp_gain.astype(jnp.bfloat16), "dp", axis=0, tiled=True),
    )
    inverse_two = rms_inverse(middle)
    gain_two = mlp_scale.astype(jnp.float32)
    normed_two = (middle * inverse_two * gain_two).astype(jnp.bfloat16)
    rows_two = lax.all_gather(normed_two, "tensor", axis=1, tiled=True).reshape(
        row_count, model_width
    )
    gate_rows = jnp.dot(rows_two, full_gate, preferred_element_type=jnp.float32)
    up_rows = jnp.dot(rows_two, full_up, preferred_element_type=jnp.float32)
    sigmoid_gate = jax.nn.sigmoid(gate_rows)
    hidden = (jax.nn.silu(gate_rows) * up_rows).astype(jnp.bfloat16)
    down_partial = jnp.dot(hidden, full_down, preferred_element_type=jnp.float32).reshape(
        seq_count, token_length, model_width
    )
    output = (
        middle
        + lax.psum_scatter(
            down_partial.astype(jnp.bfloat16), "tensor", scatter_dimension=1, tiled=True
        ).astype(jnp.float32)
    ).astype(jnp.bfloat16)
    back_gate, back_up, back_down = (full_gate, full_up, full_down)
    out_rows = lax.all_gather(cotangent, "tensor", axis=1, tiled=True).reshape(
        row_count, model_width
    )
    grad_down_flip = jnp.einsum("rd,rf->df", out_rows, hidden, preferred_element_type=jnp.float32)
    hidden_grad = jnp.einsum("rd,fd->rf", out_rows, back_down, preferred_element_type=jnp.float32)
    gate_grad = (
        hidden_grad * up_rows * sigmoid_gate * (1.0 + gate_rows * (1.0 - sigmoid_gate))
    ).astype(jnp.bfloat16)
    up_grad = (hidden_grad * gate_rows * sigmoid_gate).astype(jnp.bfloat16)
    grad_gate = jnp.einsum("rd,rf->df", rows_two, gate_grad, preferred_element_type=jnp.float32)
    grad_up = jnp.einsum("rd,rf->df", rows_two, up_grad, preferred_element_type=jnp.float32)
    norm_partial_two = jnp.einsum(
        "rf,df->rd", gate_grad, back_gate, preferred_element_type=jnp.float32
    ) + jnp.einsum("rf,df->rd", up_grad, back_up, preferred_element_type=jnp.float32)
    normed_two_grad = lax.psum_scatter(
        norm_partial_two.reshape(seq_count, token_length, model_width).astype(jnp.bfloat16),
        "tensor",
        scatter_dimension=1,
        tiled=True,
    ).astype(jnp.float32)
    passed_two, gain_grad_two = norm_back(normed_two_grad, middle, inverse_two, gain_two)
    middle_grad = cotangent.astype(jnp.float32) + passed_two
    back_query, back_key, back_value, back_out = (full_query, full_key, full_value, full_out)
    attn_rows_grad = lax.all_gather(
        middle_grad.astype(jnp.bfloat16), "tensor", axis=1, tiled=True
    ).reshape(row_count, model_width)
    grad_out_flip = jnp.einsum(
        "rd,rh->dh", attn_rows_grad, attended, preferred_element_type=jnp.float32
    )
    attended_grad = jnp.einsum(
        "rd,hd->rh", attn_rows_grad, back_out, preferred_element_type=jnp.float32
    ).astype(jnp.bfloat16)
    grad_items = split_groups(attended_grad, seq_count, local_groups).reshape(
        item_count, token_length, group_ratio, head_width
    )
    query_grad_items, key_grad_items, value_grad_items = lax.map(
        attend_backward,
        (query_items, key_items, value_items, grad_items, log_totals, segment_items),
    )
    query_joined = join_groups(
        query_grad_items.reshape(item_count, token_length, group_ratio * head_width), seq_count
    ).reshape(row_count, local_heads, head_width)
    query_grad = (
        rope_back(query_joined, cosine_table, sine_table)
        .astype(jnp.bfloat16)
        .reshape(row_count, local_heads * head_width)
    )
    key_joined = join_groups(key_grad_items, seq_count).reshape(row_count, local_groups, head_width)
    key_grad = (
        rope_back(key_joined, cosine_table, sine_table)
        .astype(jnp.bfloat16)
        .reshape(row_count, local_groups * head_width)
    )
    value_grad = join_groups(value_grad_items, seq_count).astype(jnp.bfloat16)
    grad_query = jnp.einsum("rd,rh->dh", rows_one, query_grad, preferred_element_type=jnp.float32)
    grad_key = jnp.einsum("rd,rh->dh", rows_one, key_grad, preferred_element_type=jnp.float32)
    grad_value = jnp.einsum("rd,rh->dh", rows_one, value_grad, preferred_element_type=jnp.float32)
    norm_partial_one = jnp.einsum(
        "rh,dh->rd", query_grad, back_query, preferred_element_type=jnp.float32
    )
    norm_partial_one = norm_partial_one + jnp.einsum(
        "rh,dh->rd", key_grad, back_key, preferred_element_type=jnp.float32
    )
    norm_partial_one = norm_partial_one + jnp.einsum(
        "rh,dh->rd", value_grad, back_value, preferred_element_type=jnp.float32
    )
    normed_one_grad = lax.psum_scatter(
        norm_partial_one.reshape(seq_count, token_length, model_width).astype(jnp.bfloat16),
        "tensor",
        scatter_dimension=1,
        tiled=True,
    ).astype(jnp.float32)
    passed_one, gain_grad_one = norm_back(normed_one_grad, residual, inverse_one, gain_one)
    input_grad = (middle_grad + passed_one).astype(jnp.bfloat16)
    gain_sum_one, gain_sum_two = lax.psum((gain_grad_one, gain_grad_two), "tensor")
    shards = (
        lax.psum_scatter(grad_query, "dp", scatter_dimension=0, tiled=True),
        lax.psum_scatter(grad_key, "dp", scatter_dimension=0, tiled=True),
        lax.psum_scatter(grad_value, "dp", scatter_dimension=0, tiled=True),
        lax.psum_scatter(grad_out_flip, "dp", scatter_dimension=0, tiled=True),
        lax.psum_scatter(gain_sum_one, "dp", scatter_dimension=0, tiled=True),
        lax.psum_scatter(grad_gate, "dp", scatter_dimension=0, tiled=True),
        lax.psum_scatter(grad_up, "dp", scatter_dimension=0, tiled=True),
        lax.psum_scatter(grad_down_flip, "dp", scatter_dimension=0, tiled=True),
        lax.psum_scatter(gain_sum_two, "dp", scatter_dimension=0, tiled=True),
    )
    return (
        output,
        input_grad,
        shards[0],
        shards[1],
        shards[2],
        shards[3].T,
        shards[4],
        shards[5],
        shards[6],
        shards[7].T,
        shards[8],
    )


def solution(mesh):
    in_specs = (
        P("dp", "tensor", None),
        P("dp", None),
        P("dp", None),
        P("dp", "tensor"),
        P("dp", "tensor"),
        P("dp", "tensor"),
        P("tensor", "dp"),
        P("dp"),
        P("dp", "tensor"),
        P("dp", "tensor"),
        P("tensor", "dp"),
        P("dp"),
        P("dp", "tensor", None),
    )
    out_specs = (
        P("dp", "tensor", None),
        P("dp", "tensor", None),
        P("dp", "tensor"),
        P("dp", "tensor"),
        P("dp", "tensor"),
        P("tensor", "dp"),
        P("dp"),
        P("dp", "tensor"),
        P("dp", "tensor"),
        P("tensor", "dp"),
        P("dp"),
    )
    return jax.shard_map(body, mesh=mesh, in_specs=in_specs, out_specs=out_specs, check_vma=False)
```

profile of v0, /device:TPU:0, one launch (start us, length us, event | category | flops | bytes accessed | tf_op | source)
XLA Modules:
  0.0 1690.2 jit_solution(10903615436344880350)
XLA Ops:
  12.6 36.2 %all-reduce.6 = (bf16[1536]{0:T(1024)(128)(2,1)S(1)}, bf16[1536]{0:T(1024)(128)(2,1)}) all-reduce(bf16[1536]{0:T(1024)(128)(2,1)S(1)} %dynamic-update-slice, bf16[1536]{0:T(1024)(128)(2,1)S(1)} %dynamic-update-slice.1), channel_id=1, replica_groups=mesh['dp'=16,'tensor'=2] {'dp'}, use_global_device_ids=true, to_apply=%add | all-reduce | flops 3072 | bytes 12288
  59.3 38.9 %all-gather.12.cloned.1.call-done = bf16[1,1024,1536]{2,1,0:T(8,128)(2,1)} async-done(((bf16[1,512,1536]{2,1,0:T(8,128)(2,1)}), bf16[1,1024,1536]{2,1,0:T(8,128)(2,1)}) %all-gather.12.cloned.1.call-update) | async-done | bytes 3145744 | tf_op jit(solution)/shard_map/all_gather | solution.py:201
  103.1 36.4 %all-gather.18.cloned.1.call-done = bf16[1536,384]{1,0:T(8,128)(2,1)} async-done(((bf16[96,384]{1,0:T(8,128)(2,1)}), bf16[1536,384]{1,0:T(8,128)(2,1)}) %all-gather.18.cloned.1.call-update) | async-done | bytes 1179664 | tf_op jit(solution)/shard_map/all_gather | solution.py:185
  144.0 39.5 %all-gather.14.cloned.1.call-done = bf16[1536,768]{1,0:T(8,128)(2,1)} async-done(((bf16[96,768]{1,0:T(8,128)(2,1)}), bf16[1536,768]{1,0:T(8,128)(2,1)}) %all-gather.14.cloned.1.call-update) | async-done | bytes 2359312 | tf_op jit(solution)/shard_map/all_gather | solution.py:183
  193.4 58.3 %while.54 = (s32[]{:T(128)}, bf16[4,1024,2,96]{1,3,2,0:T(8,128)(2,1)S(1)}, f32[4,2,2,512]{3,2,1,0:T(2,128)S(1)}, bf16[4,1024,2,96]{1,3,2,0:T(8,128)(2,1)}, s32[4...) while((s32[]{:T(128)}, ...), condition=%wide.region_6.7_spmd, body=%wide.region_1.6_spmd.sunk | while | flops 416906752 | bytes 19470788 | solution.py:229
  261.2 39.9 %reduce-scatter.14.cloned.1.call-done = bf16[1,512,1536]{2,1,0:T(8,128)(2,1)} async-done(((bf16[1,1024,1536]{2,1,0:T(8,128)(2,1)}), bf16[1,512,1536]{2,1,0:T(8,128)(2,1)}) %reduce-scatter.14.cloned.1.call-update) | async-done | bytes 1572880 | tf_op jit(solution)/shard_map/reduce_scatter | solution.py:238
  309.6 55.9 %all-gather.26.cloned.1.call-done = bf16[1536,2048]{1,0:T(8,128)(2,1)} async-done(((bf16[96,2048]{1,0:T(8,128)(2,1)}), bf16[1536,2048]{1,0:T(8,128)(2,1)}) %all-gather.26.cloned.1.call-update) | async-done | bytes 6291472 | tf_op jit(solution)/shard_map/all_gather | solution.py:243
  365.4 45.8 %all-gather.22.cloned.1.call-done = bf16[1,1024,1536]{2,1,0:T(8,128)(2,1)} async-done(((bf16[1,512,1536]{2,1,0:T(8,128)(2,1)}), bf16[1,1024,1536]{2,1,0:T(8,128)(2,1)}) %all-gather.22.cloned.1.call-update) | async-done | bytes 3145744 | tf_op jit(solution)/shard_map/all_gather | solution.py:250
  411.2 11.7 fusion.88
  422.9 53.3 %all-gather.24.cloned.1.call-done = bf16[1536,2048]{1,0:T(8,128)(2,1)} async-done(((bf16[96,2048]{1,0:T(8,128)(2,1)}), bf16[1536,2048]{1,0:T(8,128)(2,1)}) %all-gather.24.cloned.1.call-update) | async-done | bytes 6291472 | tf_op jit(solution)/shard_map/all_gather | solution.py:242
  476.2 11.7 fusion.90
  487.9 33.4 %all-gather.30.cloned.1.call-done = bf16[1,1024,1536]{2,1,0:T(8,128)(2,1)} async-done(((bf16[1,512,1536]{2,1,0:T(8,128)(2,1)}), bf16[1,1024,1536]{2,1,0:T(8,128)(2,1)}) %all-gather.30.cloned.1.call-update) | async-done | bytes 3145744 | tf_op jit(solution)/shard_map/all_gather | solution.py:267
  521.3 64.4 %all-gather.28.cloned.1.call-done = bf16[2048,1536]{0,1:T(8,128)(2,1)} async-done(((bf16[2048,96]{0,1:T(8,128)(2,1)}), bf16[2048,1536]{0,1:T(8,128)(2,1)}) %all-gather.28.cloned.1.call-update) | async-done | bytes 6291472 | tf_op jit(solution)/shard_map/all_gather | solution.py:244
  585.7 19.2 %multiply_convert_fusion = (bf16[1024,2048]{1,0:T(8,128)(2,1)}, bf16[1024,2048]{1,0:T(8,128)(2,1)}, bf16[1024,2048]{1,0:T(8,128)(2,1)}) fusion(f32[1024,2048]{1,0:T(8,128)} %fusion.90, f32[1024,2048]{1,0:T(8,128)} %fusion.88, bf16[2048,1536]{0,1:T(8,128)(2,1)} %all-gather.28.cloned.1.call-done, bf16[1,1024,1536]{2,1,0:T(8,128)(2,1)} %all-gather.30.cloned.1.call-done), kind=kOutput, calls=%fused_computation.74 | convolution fusion | flops 6476005376 | bytes 38797312 | tf_op jit(solution)/shard_map/rd,fd->rf/dot_general | solution.py:271
  624.0 42.0 %reduce-scatter.18.cloned.1.call-done = bf16[1,512,1536]{2,1,0:T(8,128)(2,1)} async-done(((bf16[1,1024,1536]{2,1,0:T(8,128)(2,1)}), bf16[1,512,1536]{2,1,0:T(8,128)(2,1)}) %reduce-scatter.18.cloned.1.call-update) | async-done | bytes 1572880 | tf_op jit(solution)/shard_map/reduce_scatter | solution.py:281
  672.1 45.0 %all-gather.32.cloned.1.call-done = bf16[1,1024,1536]{2,1,0:T(8,128)(2,1)} async-done(((bf16[1,512,1536]{2,1,0:T(8,128)(2,1)}), bf16[1,1024,1536]{2,1,0:T(8,128)(2,1)}) %all-gather.32.cloned.1.call-update) | async-done | bytes 3145744 | tf_op jit(solution)/shard_map/all_gather | solution.py:290
  723.5 147.1 %while.56 = (s32[]{:T(128)}, f32[4,1024,2,96]{1,3,2,0:T(8,128)}, f32[4,1024,96]{1,2,0:T(8,128)}, bf16[4,1024,96]{1,2,0:T(8,128)(2,1)}, f32[4,2,2,512]{3,2,1,0:T(...) while((s32[]{:T(128)}, f32[4,1024,2,96]{1,3,2,0:T(8,128)}, ...), condition=%wide.region_16.17_spmd, body=%wide.region_12.16_spmd.sunk | while | flops 1024523776 | bytes 65540212 | solution.py:302
  727.6 27.7 %while.58 = (s32[]{:T(128)}, f32[1024,96]{0,1:T(8,128)}, f32[1024,96]{0,1:T(8,128)}, f32[2,512,2,96]{1,3,2,0:T(8,128)}, s32[2]{0:T(128)S(1)}, /*index=5*/s32[102...) while((s32[]{:T(128)}, f32[1024,96]{0,1:T(8,128)}, ...), condition=%wide.region_15.15_spmd.clone, body=%wide.region_13.14_spmd.clone.sunk | while | flops 1024523776 | bytes 56863552 | solution.py:158
  764.3 27.7 %while.58 = (s32[]{:T(128)}, f32[1024,96]{0,1:T(8,128)}, f32[1024,96]{0,1:T(8,128)}, f32[2,512,2,96]{1,3,2,0:T(8,128)}, s32[2]{0:T(128)S(1)}, /*index=5*/s32[102...) while((s32[]{:T(128)}, f32[1024,96]{0,1:T(8,128)}, ...), condition=%wide.region_15.15_spmd.clone, body=%wide.region_13.14_spmd.clone.sunk | while | flops 1024523776 | bytes 56863552 | solution.py:158
  801.0 27.7 %while.58 = (s32[]{:T(128)}, f32[1024,96]{0,1:T(8,128)}, f32[1024,96]{0,1:T(8,128)}, f32[2,512,2,96]{1,3,2,0:T(8,128)}, s32[2]{0:T(128)S(1)}, /*index=5*/s32[102...) while((s32[]{:T(128)}, f32[1024,96]{0,1:T(8,128)}, ...), condition=%wide.region_15.15_spmd.clone, body=%wide.region_13.14_spmd.clone.sunk | while | flops 1024523776 | bytes 56863552 | solution.py:158
  837.7 27.7 %while.58 = (s32[]{:T(128)}, f32[1024,96]{0,1:T(8,128)}, f32[1024,96]{0,1:T(8,128)}, f32[2,512,2,96]{1,3,2,0:T(8,128)}, s32[2]{0:T(128)S(1)}, /*index=5*/s32[102...) while((s32[]{:T(128)}, f32[1024,96]{0,1:T(8,128)}, ...), condition=%wide.region_15.15_spmd.clone, body=%wide.region_13.14_spmd.clone.sunk | while | flops 1024523776 | bytes 56863552 | solution.py:158
  886.6 11.7 fusion.56
  924.9 11.6 fusion.86
  936.6 12.0 fusion.84
  961.9 12.7 copy.44
  978.7 60.8 %all-reduce.4 = (f32[1536]{0:T(1024)S(1)}, f32[1536]{0:T(1024)S(1)}) all-reduce(f32[1536]{0:T(1024)S(1)} %get-tuple-element.281, f32[1536]{0:T(1024)S(1)} %copy-done.29), channel_id=10, replica_groups=mesh['dp'=16,'tensor'=2] {'dp'}, use_global_device_ids=true, to_apply=%region_25.26.clone | all-reduce | flops 3072 | bytes 24576
  1051.0 58.6 %reduce-scatter.26.cloned.1.call-done = f32[96,384]{1,0:T(8,128)} async-done(((f32[1536,384]{1,0:T(8,128)}), f32[96,384]{1,0:T(8,128)}) %reduce-scatter.26.cloned.1.call-update) | async-done | bytes 147472 | tf_op jit(solution)/shard_map/reduce_scatter | solution.py:345
  1109.6 79.0 %reduce-scatter.28.cloned.1.call-done = f32[96,768]{1,0:T(8,128)} async-done(((f32[1536,768]{1,0:T(8,128)}), f32[96,768]{1,0:T(8,128)}) %reduce-scatter.28.cloned.1.call-update) | async-done | bytes 294928 | tf_op jit(solution)/shard_map/reduce_scatter | solution.py:346
  1188.5 79.5 %reduce-scatter.22.cloned.1.call-done = f32[96,768]{1,0:T(8,128)} async-done(((f32[1536,768]{1,0:T(8,128)}), f32[96,768]{1,0:T(8,128)}) %reduce-scatter.22.cloned.1.call-update) | async-done | bytes 294928 | tf_op jit(solution)/shard_map/reduce_scatter | solution.py:343
  1268.1 138.2 %reduce-scatter.30.cloned.1.call-done = f32[96,2048]{1,0:T(8,128)} async-done(((f32[1536,2048]{1,0:T(8,128)}), f32[96,2048]{1,0:T(8,128)}) %reduce-scatter.30.cloned.1.call-update) | async-done | bytes 786448 | tf_op jit(solution)/shard_map/reduce_scatter | solution.py:348
  1406.3 138.4 %reduce-scatter.32.cloned.1.call-done = f32[96,2048]{1,0:T(8,128)} async-done(((f32[1536,2048]{1,0:T(8,128)}), f32[96,2048]{1,0:T(8,128)}) %reduce-scatter.32.cloned.1.call-update) | async-done | bytes 786448 | tf_op jit(solution)/shard_map/reduce_scatter | solution.py:349
  1544.7 138.4 %reduce-scatter.34.cloned.1.call-done = f32[96,2048]{1,0:T(8,128)} async-done(((f32[1536,2048]{1,0:T(8,128)}), f32[96,2048]{1,0:T(8,128)}) %reduce-scatter.34.cloned.1.call-update) | async-done | bytes 786448
  (500 shorter events, 393.5 us)
Async XLA Ops:
  7.2 50.4 %all-gather.16.cloned.1.call-start = ((), (), s32[]{:S(2)}) async-start(), calls=%async_computation.13 | async-start | bytes 1253376 | tf_op jit(solution)/shard_map/all_gather | solution.py:184
  8.8 89.4 %all-gather.12.cloned.1.call-start = ((), (), s32[]{:S(2)}) async-start(), calls=%async_computation.11 | async-start | bytes 4718592 | tf_op jit(solution)/shard_map/all_gather | solution.py:201
  54.3 85.2 %all-gather.18.cloned.1.call-start = ((), (), s32[]{:S(2)}) async-start(), calls=%async_computation.14 | async-start | bytes 1253376 | tf_op jit(solution)/shard_map/all_gather | solution.py:185
  55.0 128.5 %all-gather.14.cloned.1.call-start = ((), (), s32[]{:S(2)}) async-start(), calls=%async_computation.12 | async-start | bytes 2506752 | tf_op jit(solution)/shard_map/all_gather | solution.py:183
  55.8 196.0 %all-gather.20.cloned.1.call-start = ((), (), s32[]{:S(2)}) async-start(), calls=%async_computation.15 | async-start | bytes 2506752 | tf_op jit(solution)/shard_map/all_gather | solution.py:186
  56.6 244.5 %reduce-scatter.14.cloned.1.call-start = ((), (), s32[]{:S(2)}) async-start(), calls=%async_computation.16 | async-start | bytes 4718592 | tf_op jit(solution)/shard_map/reduce_scatter | solution.py:238
  57.5 133.9 %copy-start.8 = (f32[1024,96]{0,1:T(8,128)}, f32[1024,96]{0,1:T(8,128)S(1)}, u32[]{:S(2)}) copy-start(f32[1024,96]{0,1:T(8,128)S(1)} %maximum_bitcast_fusion) | copy-start | bytes 1179652
  57.5 133.8 %copy-start.13 = (f32[1024,96]{0,1:T(8,128)}, f32[1024,96]{0,1:T(8,128)S(1)}, u32[]{:S(2)}) copy-start(f32[1024,96]{0,1:T(8,128)S(1)} %maximum_bitcast_fusion.1) | copy-start | bytes 1179652
  258.7 42.4 %copy-start.3 = (bf16[1,512,1536]{2,1,0:T(8,128)(2,1)S(1)}, bf16[1,512,1536]{2,1,0:T(8,128)(2,1)}, u32[]{:S(2)}) copy-start(bf16[1,512,1536]{2,1,0:T(8,128)(2,1)} %param.21) | copy-start | bytes 4718596
  258.7 106.7 %all-gather.26.cloned.1.call-start = ((), (), s32[]{:S(2)}) async-start(), calls=%async_computation.19 | async-start | bytes 6684672 | tf_op jit(solution)/shard_map/all_gather | solution.py:243
  260.7 150.5 %all-gather.22.cloned.1.call-start = ((), (), s32[]{:S(2)}) async-start(), calls=%async_computation.17 | async-start | bytes 4718592 | tf_op jit(solution)/shard_map/all_gather | solution.py:250
  261.2 408.3 %copy-start.22 = (f32[1536]{0:T(1024)}, f32[1536]{0:T(1024)S(1)}, u32[]{:S(2)}) copy-start(f32[1536]{0:T(1024)S(1)} %convert_element_type.193) | copy-start | bytes 18436
  303.2 366.3 %copy-start.27 = (f32[512]{0:T(512)}, f32[512]{0:T(512)S(1)}, u32[]{:S(2)}) copy-start(f32[512]{0:T(512)S(1)} %add_rsqrt_fusion) | copy-start | bytes 6148
  304.9 171.3 %all-gather.24.cloned.1.call-start = ((), (), s32[]{:S(2)}) async-start(), calls=%async_computation.18 | async-start | bytes 6684672 | tf_op jit(solution)/shard_map/all_gather | solution.py:242
  306.9 214.3 %all-gather.30.cloned.1.call-start = ((), (), s32[]{:S(2)}) async-start(), calls=%async_computation.22 | async-start | bytes 4718592 | tf_op jit(solution)/shard_map/all_gather | solution.py:267
  307.5 278.2 %all-gather.28.cloned.1.call-start = ((), (), s32[]{:S(2)}) async-start(), calls=%async_computation.20 | async-start | bytes 6684672 | tf_op jit(solution)/shard_map/all_gather | solution.py:244
  309.5 356.6 %reduce-scatter.18.cloned.1.call-start = ((), (), s32[]{:S(2)}) async-start(), calls=%async_computation.23 | async-start | bytes 4718592 | tf_op jit(solution)/shard_map/reduce_scatter | solution.py:281
  585.7 19.2 %copy-start.37 = (bf16[1536,2048]{1,0:T(8,128)(2,1)S(1)}, bf16[1536,2048]{1,0:T(8,128)(2,1)}, u32[]{:S(2)}) copy-start(bf16[1536,2048]{1,0:T(8,128)(2,1)} %all-gather.24.cloned.1.call-done) | copy-start | bytes 18874372
  624.0 93.1 %all-gather.32.cloned.1.call-start = ((), (), s32[]{:S(2)}) async-start(), calls=%async_computation.24 | async-start | bytes 4718592 | tf_op jit(solution)/shard_map/all_gather | solution.py:290
  672.0 303.5 %reduce-scatter.20.cloned.1.call-start = ((), (), s32[]{:S(2)}) async-start(), calls=%async_computation.25 | async-start | bytes 4718592 | tf_op jit(solution)/shard_map/reduce_scatter | solution.py:333
  886.6 158.5 %reduce-scatter.16.cloned.1.call-start = ((), (), s32[]{:S(2)}) async-start(), calls=%async_computation.21 | async-start | bytes 4718592 | tf_op jit(solution)/shard_map/reduce_scatter | solution.py:262
  898.4 152.7 %reduce-scatter.24.cloned.1.call-start = ((), (), s32[]{:S(2)}) async-start(), calls=%async_computation.27 | async-start | bytes 2506752 | tf_op jit(solution)/shard_map/reduce_scatter | solution.py:344
  903.6 205.9 %reduce-scatter.26.cloned.1.call-start = ((), (), s32[]{:S(2)}) async-start(), calls=%async_computation.28 | async-start | bytes 2506752 | tf_op jit(solution)/shard_map/reduce_scatter | solution.py:345
  909.0 279.5 %reduce-scatter.28.cloned.1.call-start = ((), (), s32[]{:S(2)}) async-start(), calls=%async_computation.29 | async-start | bytes 5013504 | tf_op jit(solution)/shard_map/reduce_scatter | solution.py:346
  916.3 351.8 %reduce-scatter.22.cloned.1.call-start = ((), (), s32[]{:S(2)}) async-start(), calls=%async_computation.26 | async-start | bytes 5013504 | tf_op jit(solution)/shard_map/reduce_scatter | solution.py:343
  923.1 483.2 %reduce-scatter.30.cloned.1.call-start = ((), (), s32[]{:S(2)}) async-start(), calls=%async_computation.30 | async-start | bytes 13369344 | tf_op jit(solution)/shard_map/reduce_scatter | solution.py:348
  936.5 608.2 %reduce-scatter.32.cloned.1.call-start = ((), (), s32[]{:S(2)}) async-start(), calls=%async_computation.31 | async-start | bytes 13369344 | tf_op jit(solution)/shard_map/reduce_scatter | solution.py:349
  948.7 734.5 %reduce-scatter.34.cloned.1.call-start = ((), (), s32[]{:S(2)}) async-start(), calls=%async_computation.32 | async-start | bytes 13369344
  974.6 70.4 %copy-start.6 = (bf16[1,512,1536]{2,1,0:T(8,128)(2,1)S(1)}, bf16[1,512,1536]{2,1,0:T(8,128)(2,1)}, u32[]{:S(2)}) copy-start(bf16[1,512,1536]{2,1,0:T(8,128)(2,1)} %reduce-scatter.14.cloned.1.call-done) | copy-start | bytes 4718596
  974.7 70.4 %copy-start.23 = (f32[1536]{0:T(1024)S(1)}, f32[1536]{0:T(1024)}, u32[]{:S(2)}) copy-start(f32[1536]{0:T(1024)} %copy-done.22) | copy-start | bytes 18436
  974.7 70.4 %copy-start.28 = (f32[512]{0:T(512)S(1)}, f32[512]{0:T(512)}, u32[]{:S(2)}) copy-start(f32[512]{0:T(512)} %copy-done.27) | copy-start | bytes 6148
  974.7 70.4 %copy-start.33 = (f32[512]{0:T(512)S(1)}, f32[512]{0:T(512)}, u32[]{:S(2)}) copy-start(f32[512]{0:T(512)} %copy-done.32) | copy-start | bytes 6148
  (54 other events, 170.6 us)
Sparse Core Ops, SparseCore 0:
  10.9 41.0 all-gather.15
  54.4 43.7 all-gather.11
  101.1 38.3 all-gather.17
  142.2 41.2 all-gather.13
  186.2 41.1 all-gather.19
  258.8 42.1 reduce-scatter.13
  303.6 61.8 all-gather.25
  367.6 43.5 all-gather.21
  414.3 61.8 all-gather.23
  477.7 43.5 all-gather.29
  523.8 61.8 all-gather.27
  624.1 41.9 reduce-scatter.17
  672.1 44.9 all-gather.31
  886.7 43.3 reduce-scatter.19
  932.2 43.3 reduce-scatter.15
  979.8 63.1 reduce-scatter.23
  1047.6 61.9 reduce-scatter.25
  1113.9 74.6 reduce-scatter.27
  1193.5 74.5 reduce-scatter.21
  1272.5 133.7 reduce-scatter.29
  1410.9 133.7 reduce-scatter.31
  1549.3 133.7 reduce-scatter.33
where the time goes:
time: 1700 us; the launch traced here: 1690 us
  waiting for transfers between devices  1130 us (66%)
  matrix products  267 us (16%)
  blocking collectives  102 us (6%)
  local copies, waits for them, and re-layouts  90.5 us (5%)
  other arithmetic  72.8 us (4%)
    unnamed x23, waiting for transfers between devices  139 us
    reduce_scatter x1, waiting for transfers between devices, body(): lax.psum_scatter(grad_up, 'dp', scatter_dimension=0, tiled=True)  138 us
    reduce_scatter x1, waiting for transfers between devices, body(): lax.psum_scatter(grad_gate, 'dp', scatter_dimension=0, tiled=True)  138 us
    unnamed x2, blocking collectives  96.9 us
    reduce_scatter x1, waiting for transfers between devices, body(): lax.psum_scatter(grad_query, 'dp', scatter_dimension=0, tiled=True)  79.5 us
    reduce_scatter x1, waiting for transfers between devices, body(): lax.psum_scatter(grad_out_flip, 'dp', scatter_dimension=0, tiled=True)  79 us
    all_gather x1, waiting for transfers between devices, body(): lax.all_gather(down_weight.astype(jnp.bfloat16), 'dp', axis=1, tiled=True)  64.4 us
    reduce_scatter x1, waiting for transfers between devices, body(): lax.psum_scatter(grad_value, 'dp', scatter_dimension=0, tiled=True)  58.6 us
  transfers between devices with their start and end apart: 22, of which 17 were waited for; matrix products, arithmetic and copies ran while one was open for 12% of the time, Pallas kernels for 0%

commit v1 on v0

v1 whole, which is shorter than its diff:
```python
import functools
import math

import jax
import jax.numpy as jnp
from jax import lax
from jax.experimental import pallas as pl
from jax.experimental.pallas import tpu as pltpu
from jax.sharding import PartitionSpec as P

HEAD_DIM = 96
PAD_DIM = 128
BLOCK = 256
DOCS = 16
EPSILON = 1e-05
ROPE_BASE = 100000.0
FAR = float(2**30)
RING_LIMIT = 16
SCALE = 1.0 / math.sqrt(HEAD_DIM)
LOG2E = math.log2(math.e)

F32 = jnp.float32
BF16 = jnp.bfloat16


def mm(left, right, left_dim, right_dim, dtype=F32):
    return lax.dot_general(
        left, right, (((left_dim,), (right_dim,)), ((), ())), preferred_element_type=F32
    ).astype(dtype)


def swap_halves(value):
    return lax.ppermute(value, "tensor", [(0, 1), (1, 0)])


def ring_of(dp):
    chips = dp // 2
    order = list(range(0, chips, 2)) + list(range(chips - 1 - chips % 2, 0, -2))
    place = [0] * chips
    for spot, chip in enumerate(order):
        place[chip] = spot
    pairs = []
    for spot in range(chips):
        here, after = order[spot], order[(spot + 1) % chips]
        pairs.append((2 * here, 2 * after))
        pairs.append((2 * after + 1, 2 * here + 1))
    return order, place, pairs


def ring_state(dp):
    order, place, pairs = ring_of(dp)
    chips = dp // 2
    me = lax.axis_index("dp")
    core = me % 2
    spot = jnp.asarray(place, jnp.int32)[me // 2]
    order = jnp.asarray(order, jnp.int32)

    def chip_at(steps, which):
        shift = jnp.where(which == 0, steps, -steps)
        return order[(spot + shift + 2 * chips) % chips]

    return me, core, chip_at, pairs


def gather_rows(shard, dp):
    if dp > RING_LIMIT or dp < 4:
        return lax.all_gather(shard, "dp", axis=0, tiled=True)
    rows = shard.shape[0]
    me, core, chip_at, pairs = ring_state(dp)
    swap = [(i, i ^ 1) for i in range(dp)]
    whole = jnp.zeros((dp * rows, shard.shape[1]), shard.dtype)

    def put(whole, piece, device):
        return lax.dynamic_update_slice(whole, piece, (device * rows, 0))

    held = shard
    for step in range(dp // 2):
        if step:
            held = lax.ppermute(held, "dp", pairs)
        other = lax.ppermute(held, "dp", swap)
        whole = put(whole, held, 2 * chip_at(-step, core) + core)
        whole = put(whole, other, 2 * chip_at(-step, 1 - core) + 1 - core)
    return whole


def scatter_rows(full, dp):
    if dp > RING_LIMIT or dp < 4:
        return lax.psum_scatter(full, "dp", scatter_dimension=0, tiled=True).astype(F32)
    rows = full.shape[0] // dp
    width = full.shape[1]
    chips = dp // 2
    me, core, chip_at, pairs = ring_state(dp)
    swap = [(i, i ^ 1) for i in range(dp)]
    parts = full.reshape(chips, 2, rows, width)
    mine = lax.dynamic_slice(parts, (0, core, 0, 0), (chips, 1, rows, width))[:, 0]
    theirs = lax.dynamic_slice(parts, (0, 1 - core, 0, 0), (chips, 1, rows, width))[:, 0]
    got = lax.ppermute(theirs, "dp", swap)

    def local(steps):
        chip = chip_at(steps, core)
        both = [lax.dynamic_slice(a, (chip, 0, 0), (1, rows, width))[0] for a in (mine, got)]
        return both[0].astype(F32) + both[1].astype(F32)

    total = local(-1)
    for step in range(2, chips + 1):
        held = lax.ppermute(total.astype(BF16), "dp", pairs)
        total = held.astype(F32) + local(-step)
    return total


def place_of(natural, side, length):
    return pl.multiple_of((natural + side * (length // 2)) % length, BLOCK)


def rope_rows(top, bottom, cos, sin):
    return top * cos - bottom * sin, bottom * cos + top * sin


def diagonal():
    keys = lax.broadcasted_iota(jnp.int32, (BLOCK, BLOCK), 0)
    queries = lax.broadcasted_iota(jnp.int32, (BLOCK, BLOCK), 1)
    return keys <= queries


def forward_kernel(
    side_ref, q_in, k_in, v_in, cos_ref, sin_ref, oq_ref, ok_ref,
    att_ref, q_out, k_out, v_out, lse_ref, q_scr, kt_scr, k_scr,
):
    length = q_in.shape[1]
    half = HEAD_DIM // 2
    side = side_ref[0]
    blocks = length // BLOCK
    kt_scr[HEAD_DIM:, :] = jnp.zeros((PAD_DIM - HEAD_DIM, length), BF16)
    kt_scr[HEAD_DIM : HEAD_DIM + DOCS, :] = ok_ref[...]
    for h in range(2):
        q_scr[h, HEAD_DIM:, :] = jnp.zeros((PAD_DIM - HEAD_DIM, length), BF16)
        q_scr[h, HEAD_DIM : HEAD_DIM + DOCS, :] = oq_ref[...]
    for b in range(blocks):
        here = pl.ds(b * BLOCK, BLOCK)
        there = pl.ds(place_of(b * BLOCK, side, length), BLOCK)
        cos, sin = cos_ref[:, there], sin_ref[:, there]
        for source, row, target in (
            (q_in, 0, q_scr.at[0]),
            (q_in, HEAD_DIM, q_scr.at[1]),
            (k_in, 0, kt_scr),
        ):
            top, bottom = rope_rows(
                source[row : row + half, there], source[row + half : row + HEAD_DIM, there], cos, sin
            )
            target[:half, here] = top.astype(BF16)
            target[half:HEAD_DIM, here] = bottom.astype(BF16)
        v_out[:, here] = v_in[:, there].astype(BF16)
    for h in range(2):
        q_out[h * HEAD_DIM : (h + 1) * HEAD_DIM, :] = q_scr[h, :HEAD_DIM, :]
    k_out[...] = kt_scr[:HEAD_DIM, :]
    k_scr[...] = kt_scr[...].T
    causal = diagonal()
    for h in range(2):
        for b in range(blocks):
            here = pl.ds(b * BLOCK, BLOCK)
            keys = (b + 1) * BLOCK
            query = q_scr[h, :, here]
            last = mm(k_scr[b * BLOCK : keys, :], query, 1, 0)
            last = jnp.where(causal, last, -FAR)
            top = jnp.max(last, 0, keepdims=True)
            if b:
                early = mm(k_scr[: b * BLOCK, :], query, 1, 0)
                top = jnp.maximum(top, jnp.max(early, 0, keepdims=True))
            top = top * (SCALE * LOG2E)
            weight = jnp.exp2(last * (SCALE * LOG2E) - top)
            total = jnp.sum(weight, 0, keepdims=True)
            out = mm(v_out[:, b * BLOCK : keys], weight.astype(BF16), 1, 0)
            if b:
                weight = jnp.exp2(early * (SCALE * LOG2E) - top)
                total = total + jnp.sum(weight, 0, keepdims=True)
                out = out + mm(v_out[:, : b * BLOCK], weight.astype(BF16), 1, 0)
            out = out / total
            there = pl.ds(place_of(b * BLOCK, side, length), BLOCK)
            att_ref[h * HEAD_DIM : (h + 1) * HEAD_DIM, there] = out.astype(BF16)
            lse_ref[0, h : h + 1, here] = top + jnp.log2(total)


def attend(side, qkv, cos, sin, doc_q, doc_k):
    hidden, length = qkv.shape
    groups = hidden // (4 * HEAD_DIM)
    whole = lambda g, s: (0, 0)
    spec = pl.BlockSpec
    return pl.pallas_call(
        forward_kernel,
        grid_spec=pltpu.PrefetchScalarGridSpec(
            num_scalar_prefetch=1,
            grid=(groups,),
            in_specs=[
                spec((2 * HEAD_DIM, length), lambda g, s: (g, 0)),
                spec((HEAD_DIM, length), lambda g, s: (2 * groups + g, 0)),
                spec((HEAD_DIM, length), lambda g, s: (3 * groups + g, 0)),
                spec((HEAD_DIM // 2, length), whole),
                spec((HEAD_DIM // 2, length), whole),
                spec((DOCS, length), whole),
                spec((DOCS, length), whole),
            ],
            out_specs=[
                spec((2 * HEAD_DIM, length), lambda g, s: (g, 0)),
                spec((2 * HEAD_DIM, length), lambda g, s: (g, 0)),
                spec((HEAD_DIM, length), lambda g, s: (g, 0)),
                spec((HEAD_DIM, length), lambda g, s: (g, 0)),
                spec((1, 2, length), lambda g, s: (g, 0, 0)),
            ],
            scratch_shapes=[
                pltpu.VMEM((2, PAD_DIM, length), BF16),
                pltpu.VMEM((PAD_DIM, length), BF16),
                pltpu.VMEM((length, PAD_DIM), BF16),
            ],
        ),
        out_shape=[
            jax.ShapeDtypeStruct((2 * groups * HEAD_DIM, length), BF16),
            jax.ShapeDtypeStruct((2 * groups * HEAD_DIM, length), BF16),
            jax.ShapeDtypeStruct((groups * HEAD_DIM, length), BF16),
            jax.ShapeDtypeStruct((groups * HEAD_DIM, length), BF16),
            jax.ShapeDtypeStruct((groups, 2, length), F32),
        ],
        compiler_params=pltpu.CompilerParams(vmem_limit_bytes=48 * 2**20),
        cost_estimate=pl.CostEstimate(
            flops=groups * 4 * length * length * 192, bytes_accessed=12 * 2**20,
            transcendentals=groups * length * length,
        ),
        name="attend",
    )(side, qkv, qkv, qkv, cos, sin, doc_q, doc_k)


def backward_kernel(
    side_ref, q_ref, k_ref, v_ref, att_ref, datt_ref, lse_ref, cos_ref, sin_ref, oq_ref, ok_ref,
    dq_ref, dk_ref, dv_ref, q_scr, kt_scr, k_scr, vt_scr, v_scr, do_scr, dq_scr, dk_scr, dv_scr,
):
    length = q_ref.shape[1]
    half = HEAD_DIM // 2
    side = side_ref[0]
    blocks = length // BLOCK
    blank = jnp.zeros((PAD_DIM - HEAD_DIM, length), BF16)
    kt_scr[:HEAD_DIM, :] = k_ref[...]
    kt_scr[HEAD_DIM:, :] = blank
    kt_scr[HEAD_DIM : HEAD_DIM + DOCS, :] = ok_ref[...]
    vt_scr[:HEAD_DIM, :] = v_ref[...]
    vt_scr[HEAD_DIM:, :] = blank
    k_scr[...] = kt_scr[...].T
    v_scr[...] = vt_scr[...].T
    causal = diagonal()
    for h in range(2):
        rows = slice(h * HEAD_DIM, (h + 1) * HEAD_DIM)
        q_scr[:HEAD_DIM, :] = q_ref[rows, :]
        q_scr[HEAD_DIM:, :] = blank
        q_scr[HEAD_DIM : HEAD_DIM + DOCS, :] = oq_ref[...]
        do_scr[HEAD_DIM:, :] = blank
        for b in range(blocks):
            here = pl.ds(b * BLOCK, BLOCK)
            there = pl.ds(place_of(b * BLOCK, side, length), BLOCK)
            do_scr[:HEAD_DIM, here] = datt_ref[rows, there]
            base = jnp.sum(
                datt_ref[rows, there].astype(F32) * att_ref[rows, there].astype(F32), 0, keepdims=True
            )
            keys = (b + 1) * BLOCK
            query, upstream = q_scr[:, here], do_scr[:, here]
            level = lse_ref[0, h : h + 1, here]
            dq = None
            for start, stop in ((b * BLOCK, keys), (0, b * BLOCK)):
                if start == stop:
                    continue
                span = slice(start, stop)
                score = mm(k_scr[span, :], query, 1, 0)
                prob = jnp.exp2(score * (SCALE * LOG2E) - level)
                if start:
                    prob = jnp.where(causal, prob, 0.0)
                elif stop == keys:
                    prob = jnp.where(causal, prob, 0.0)
                slope = mm(v_scr[span, :], upstream, 1, 0)
                ds = (prob * (slope - base)).astype(BF16)
                part = mm(kt_scr[:HEAD_DIM, span], ds, 1, 0)
                dq = part if dq is None else dq + part
                dk = mm(query[:HEAD_DIM, :], ds, 1, 1)
                dv = mm(upstream[:HEAD_DIM, :], prob.astype(BF16), 1, 1)
                if h == 0 and start == b * BLOCK:
                    dk_scr[:, span] = dk
                    dv_scr[:, span] = dv
                else:
                    dk_scr[:, span] += dk
                    dv_scr[:, span] += dv
            cos, sin = cos_ref[:, there], sin_ref[:, there]
            dq = dq * SCALE
            top, bottom = rope_rows(dq[:half, :], dq[half:, :], cos, -sin)
            dq_ref[h * HEAD_DIM : h * HEAD_DIM + half, there] = top.astype(BF16)
            dq_ref[h * HEAD_DIM + half : (h + 1) * HEAD_DIM, there] = bottom.astype(BF16)
    for b in range(blocks):
        here = pl.ds(b * BLOCK, BLOCK)
        there = pl.ds(place_of(b * BLOCK, side, length), BLOCK)
        cos, sin = cos_ref[:, there], sin_ref[:, there]
        dk = dk_scr[:, here] * SCALE
        top, bottom = rope_rows(dk[:half, :], dk[half:, :], cos, -sin)
        dk_ref[:half, there] = top.astype(BF16)
        dk_ref[half:, there] = bottom.astype(BF16)
        dv_ref[:, there] = dv_scr[:, here].astype(BF16)


def attend_back(side, q, k, v, att, datt, lse, cos, sin, doc_q, doc_k):
    length = q.shape[1]
    groups = k.shape[0] // HEAD_DIM
    whole = lambda g, s: (0, 0)
    spec = pl.BlockSpec
    wide = spec((2 * HEAD_DIM, length), lambda g, s: (g, 0))
    narrow = spec((HEAD_DIM, length), lambda g, s: (g, 0))
    table = spec((HEAD_DIM // 2, length), whole)
    docs = spec((DOCS, length), whole)
    return pl.pallas_call(
        backward_kernel,
        grid_spec=pltpu.PrefetchScalarGridSpec(
            num_scalar_prefetch=1,
            grid=(groups,),
            in_specs=[
                wide, narrow, narrow, wide, wide, spec((1, 2, length), lambda g, s: (g, 0, 0)),
                table, table, docs, docs,
            ],
            out_specs=[wide, narrow, narrow],
            scratch_shapes=[
                pltpu.VMEM((PAD_DIM, length), BF16),
                pltpu.VMEM((PAD_DIM, length), BF16),
                pltpu.VMEM((length, PAD_DIM), BF16),
                pltpu.VMEM((PAD_DIM, length), BF16),
                pltpu.VMEM((length, PAD_DIM), BF16),
                pltpu.VMEM((PAD_DIM, length), BF16),
                pltpu.VMEM((HEAD_DIM, length), F32),
                pltpu.VMEM((HEAD_DIM, length), F32),
                pltpu.VMEM((HEAD_DIM, length), F32),
            ],
        ),
        out_shape=[
            jax.ShapeDtypeStruct(q.shape, BF16),
            jax.ShapeDtypeStruct(k.shape, BF16),
            jax.ShapeDtypeStruct(v.shape, BF16),
        ],
        compiler_params=pltpu.CompilerParams(vmem_limit_bytes=48 * 2**20),
        cost_estimate=pl.CostEstimate(
            flops=groups * 10 * length * length * 192, bytes_accessed=12 * 2**20,
            transcendentals=groups * length * length,
        ),
        name="attend_back",
    )(side, q, k, v, att, datt, lse, cos, sin, doc_q, doc_k)


def rms_inverse(value):
    return lax.rsqrt(jnp.mean(value * value, -1, keepdims=True) + EPSILON)


def norm_back(upstream, value, inverse, gain):
    scaled = upstream * gain
    inner = jnp.mean(scaled * value, -1, keepdims=True)
    return inverse * (scaled - value * inverse * inverse * inner)


def layer(
    dp, tokens, segment_ids, positions, query_weight, key_weight, value_weight, out_weight,
    attn_gain, gate_weight, up_weight, down_weight, mlp_gain, cotangent,
):
    seqs, own_rows, model = tokens.shape
    length = segment_ids.shape[1]
    heads = query_weight.shape[1]
    qkv_width = 2 * heads
    ff = gate_weight.shape[1]
    side_index = lax.axis_index("tensor").astype(jnp.int32)
    side = side_index[None]

    x_own = tokens.reshape(own_rows, model)
    e_own = cotangent.reshape(own_rows, model)
    x_par = swap_halves(x_own)
    e_par = swap_halves(e_own)

    low = lambda w: w.astype(BF16)
    gains = jnp.pad(jnp.stack([low(attn_gain), low(mlp_gain)], 1), ((0, 0), (0, 126)))
    first = gather_rows(
        jnp.concatenate(
            [low(query_weight), low(key_weight), low(value_weight), low(out_weight).T, gains], 1
        ),
        dp,
    )
    second = gather_rows(
        jnp.concatenate([low(gate_weight), low(up_weight), low(down_weight).T], 1), dp
    )
    qkv_full = first[:, :qkv_width]
    out_full = first[:, qkv_width : qkv_width + heads]
    gain_one = first[:, qkv_width + heads].astype(F32)
    gain_two = first[:, qkv_width + heads + 1].astype(F32)
    gate_full, up_full, down_full = (second[:, i * ff : (i + 1) * ff] for i in range(3))

    x = jnp.concatenate([x_own, x_par], 0).astype(F32)
    inverse_one = rms_inverse(x)
    normed_one = (x * inverse_one * gain_one).astype(BF16)

    places = positions.reshape(length).astype(F32)
    half = HEAD_DIM // 2
    places = jnp.where(side_index == 0, places, jnp.roll(places, length // 2))
    ladder = jnp.power(F32(ROPE_BASE), -2.0 * jnp.arange(half, dtype=F32) / HEAD_DIM)
    angles = ladder[:, None] * places[None, :]
    cos, sin = jnp.cos(angles), jnp.sin(angles)
    known = jnp.arange(DOCS, dtype=jnp.int32)[:, None] == segment_ids.reshape(1, length)
    doc_q = known.astype(BF16)
    doc_k = jnp.where(known, 0.0, -FAR).astype(BF16)

    qkv = mm(qkv_full, normed_one, 0, 1)
    att, q, k, v, lse = attend(side, qkv, cos, sin, doc_q, doc_k)

    sent = swap_halves(mm(att[:, own_rows:], out_full, 0, 1, BF16))
    middle = x_own.astype(F32) + (mm(att[:, :own_rows], out_full, 0, 1) + sent.astype(F32))
    inverse_two = rms_inverse(middle)
    b_own = (middle * inverse_two * gain_two).astype(BF16)
    b = jnp.concatenate([b_own, swap_halves(b_own)], 0)
    e = jnp.concatenate([e_own, e_par], 0)

    gate = mm(b, gate_full, 1, 0)
    up = mm(b, up_full, 1, 0)
    sig = jax.nn.sigmoid(gate)
    silu = gate * sig
    hidden = (silu * up).astype(BF16)
    dhid = mm(e, down_full, 1, 0)
    dgate = (dhid * up * (sig * (1.0 + gate * (1.0 - sig)))).astype(BF16)
    dup = (dhid * silu).astype(BF16)

    def db_of(rows):
        return mm(dgate[rows], gate_full, 1, 1) + mm(dup[rows], up_full, 1, 1)

    own, par = slice(0, own_rows), slice(own_rows, None)
    db_sent = swap_halves(db_of(par).astype(BF16))
    db = db_of(own) + db_sent.astype(F32)
    dh = e_own.astype(F32) + norm_back(db, middle, inverse_two, gain_two)
    gain_two_grad = jnp.sum(db * middle * inverse_two, 0)
    eh_own = dh.astype(BF16)
    eh = jnp.concatenate([eh_own, swap_halves(eh_own)], 0)

    down_sent = swap_halves(mm(hidden[par], down_full, 1, 1, BF16))
    output = (middle + (mm(hidden[own], down_full, 1, 1) + down_sent.astype(F32))).astype(BF16)

    grad_down = scatter_rows(mm(e, hidden, 0, 0, BF16), dp)
    grad_gate = scatter_rows(mm(b, dgate, 0, 0, BF16), dp)
    grad_up = scatter_rows(mm(b, dup, 0, 0, BF16), dp)

    datt = mm(out_full, eh, 0, 1, BF16)
    grad_out = mm(eh, att, 0, 1, BF16)
    dq, dk, dv = attend_back(side, q, k, v, att, datt, lse, cos, sin, doc_q, doc_k)
    dqkv = jnp.concatenate([dq, dk, dv], 0)
    grad_qkv = mm(normed_one, dqkv, 0, 1, BF16)
    da_par = mm(dqkv[:, own_rows:], qkv_full, 0, 1)
    da_own = mm(dqkv[:, :own_rows], qkv_full, 0, 1)
    scaled = x * inverse_one
    gain_one_grad = jnp.sum(da_own * scaled[own], 0) + jnp.sum(da_par * scaled[par], 0)
    gain_grads = jnp.pad(jnp.stack([gain_one_grad, gain_two_grad], 1), ((0, 0), (0, 126)))
    da = da_own + swap_halves(da_par.astype(BF16)).astype(F32)
    input_grad = (dh + norm_back(da, x[own], inverse_one[own], gain_one)).astype(BF16)

    last = scatter_rows(jnp.concatenate([grad_qkv, grad_out, gain_grads.astype(BF16)], 1), dp)
    gain_shard = last[:, qkv_width + heads :]
    gain_shard = gain_shard + swap_halves(gain_shard)
    kv = heads // 2
    return (
        output.reshape(seqs, own_rows, model),
        input_grad.reshape(seqs, own_rows, model),
        last[:, :heads],
        last[:, heads : heads + kv],
        last[:, heads + kv : qkv_width],
        last[:, qkv_width : qkv_width + heads].T,
        gain_shard[:, 0],
        grad_gate,
        grad_up,
        grad_down.T,
        gain_shard[:, 1],
    )


def solution(mesh):
    in_specs = (
        P("dp", "tensor", None),
        P("dp", None),
        P("dp", None),
        P("dp", "tensor"),
        P("dp", "tensor"),
        P("dp", "tensor"),
        P("tensor", "dp"),
        P("dp"),
        P("dp", "tensor"),
        P("dp", "tensor"),
        P("tensor", "dp"),
        P("dp"),
        P("dp", "tensor", None),
    )
    out_specs = (
        P("dp", "tensor", None),
        P("dp", "tensor", None),
        P("dp", "tensor"),
        P("dp", "tensor"),
        P("dp", "tensor"),
        P("tensor", "dp"),
        P("dp"),
        P("dp", "tensor"),
        P("dp", "tensor"),
        P("tensor", "dp"),
        P("dp"),
    )
    return jax.shard_map(
        functools.partial(layer, mesh.shape["dp"]),
        mesh=mesh,
        in_specs=in_specs,
        out_specs=out_specs,
        check_vma=False,
    )
```

time: 1700 us -> 772 us (0.45)
  waiting for transfers between devices: 1130 us -> 170 us
  local copies, waits for them, and re-layouts: 90.5 us -> 208 us
  matrix products: 267 us -> 150 us
  blocking collectives: 102 us -> 0 us
  starting transfers between devices: 1.32 us -> 89.8 us
  Pallas kernels: 0 us -> 35.1 us
  between operations: 16.6 us -> 38 us
    reduce_scatter x10 -> x0, waiting for transfers between devices: 576 us -> none  [the longest x1 138 us: body(): lax.psum_scatter(grad_up, 'dp', scatter_dimension=0, tiled=True)]
    all_gather x11 -> x0, waiting for transfers between devices: 413 us -> none  [the longest x1 64.4 us: body(): lax.all_gather(down_weight.astype(jnp.bfloat16), 'dp', axis=1, tiled=True)]
    ppermute x0 -> x71, waiting for transfers between devices: none -> 170 us  [the longest x9 83.1 us: swap_halves(): return lax.ppermute(value, 'tensor', [(0, 1), (1, 0)])]
    unnamed x23 -> x0, waiting for transfers between devices: 139 us -> none
    dynamic_update_slice x24 -> x31, local copies, waits for them, and re-layouts: 15.6 us -> 147 us  [put(): return lax.dynamic_update_slice(whole, piece, (device * rows, 0))]
    dot_general x77 -> x20, matrix products: 267 us -> 150 us  [mm(): lax.dot_general(left, right, (((left_dim,), (right_dim,)), ((), ())), pre...]
    unnamed x2 -> x0, blocking collectives: 96.9 us -> none
    ppermute x0 -> x71, starting transfers between devices: none -> 89.8 us  [the longest x28 53.5 us: scatter_rows(): held = lax.ppermute(total.astype(BF16), 'dp', pairs)]
  transfers between devices with their start and end apart: 22 -> 71, of which waited for: 17 -> 21; matrix products, arithmetic and copies ran while one was open for 12% -> 47% of each run, Pallas kernels for 0% -> 5%
where the time goes in v1:
time: 772 us; the launch traced here: 759 us
  local copies, waits for them, and re-layouts  208 us (27%)
  waiting for transfers between devices  170 us (22%)
  matrix products  150 us (19%)
  starting transfers between devices  89.8 us (12%)
  other arithmetic  68.3 us (9%)
  between operations  38 us (5%)
  Pallas kernels  35.1 us (5%)
    dot_general x20, matrix products, mm(): lax.dot_general(left, right, (((left_dim,), (right_dim,)), ((), ())), pre...  150 us
    dynamic_update_slice x31, local copies, waits for them, and re-layouts, put(): return lax.dynamic_update_slice(whole, piece, (device * rows, 0))  147 us
    ppermute x9, waiting for transfers between devices, swap_halves(): return lax.ppermute(value, 'tensor', [(0, 1), (1, 0)])  83.1 us
    ppermute x28, starting transfers between devices, scatter_rows(): held = lax.ppermute(total.astype(BF16), 'dp', pairs)  53.5 us
    ppermute x14, waiting for transfers between devices, gather_rows(): held = lax.ppermute(held, 'dp', pairs)  48.1 us
    ppermute x28, waiting for transfers between devices, scatter_rows(): held = lax.ppermute(total.astype(BF16), 'dp', pairs)  38.1 us
    convert_element_type x28, other arithmetic, scatter_rows(): held = lax.ppermute(total.astype(BF16), 'dp', pairs)  29.4 us
    pallas_call x1, Pallas kernels, attend_back(): pl.pallas_call(backward_kernel, grid_spec=pltpu.PrefetchScalarGridSpec(nu...  20.2 us
  transfers between devices with their start and end apart: 71, of which 21 were waited for; matrix products, arithmetic and copies ran while one was open for 47% of the time, Pallas kernels for 5%

profile of v1, /device:TPU:0, one launch (start us, length us, event | category | flops | bytes accessed | tf_op | source)
XLA Modules:
  0.0 758.8 jit_solution(7279955695668523722)
XLA Ops:
  33.1 15.5 %collective-permute-done.1 = bf16[96,2432]{1,0:T(8,128)(2,1)} collective-permute-done((bf16[96,2432]{1,0:T(8,128)(2,1)S(1)}, bf16[96,2432]{1,0:T(8,128)(2,1)}, u32[]{:S(2)}, u32[]{:S(2)}) %collective-permute-start.1) | collective-permute-done | bytes 466976 | tf_op jit(solution)/shard_map/ppermute | solution.py:79
  87.8 7.8 %dynamic_update_slice.97 = bf16[1536,2432]{0,1:T(8,128)(2,1)} dynamic-update-slice(bf16[1536,2432]{0,1:T(8,128)(2,1)} %dynamic_update_slice.96, bf16[96,2432]{0,1:T(8,128)(2,1)S(1)} %copy.48, s32[]{:T(128)S(6)} %select_n.890, s32[]{:T(128)} %constant.1034.clone.1) | dynamic-update-slice | bytes 933892 | tf_op jit(solution)/shard_map/dynamic_update_slice | solution.py:74
  96.9 7.8 %dynamic_update_slice.98 = bf16[1536,2432]{0,1:T(8,128)(2,1)} dynamic-update-slice(bf16[1536,2432]{0,1:T(8,128)(2,1)} %dynamic_update_slice.97, bf16[96,2432]{0,1:T(8,128)(2,1)S(1)} %copy.49, s32[]{:T(128)S(6)} %select_n.894, s32[]{:T(128)} %constant.1034.clone.1) | dynamic-update-slice | bytes 933892 | tf_op jit(solution)/shard_map/dynamic_update_slice | solution.py:74
  106.1 7.8 %dynamic_update_slice.99 = bf16[1536,2432]{0,1:T(8,128)(2,1)} dynamic-update-slice(bf16[1536,2432]{0,1:T(8,128)(2,1)} %dynamic_update_slice.98, bf16[96,2432]{0,1:T(8,128)(2,1)S(1)} %copy.50, s32[]{:T(128)S(6)} %select_n.898, s32[]{:T(128)} %constant.1034.clone.1) | dynamic-update-slice | bytes 933892 | tf_op jit(solution)/shard_map/dynamic_update_slice | solution.py:74
  115.2 7.8 %dynamic_update_slice.100 = bf16[1536,2432]{0,1:T(8,128)(2,1)} dynamic-update-slice(bf16[1536,2432]{0,1:T(8,128)(2,1)} %dynamic_update_slice.99, bf16[96,2432]{0,1:T(8,128)(2,1)S(1)} %copy.51, s32[]{:T(128)S(6)} %select_n.902, s32[]{:T(128)} %constant.1034.clone.1) | dynamic-update-slice | bytes 933892 | tf_op jit(solution)/shard_map/dynamic_update_slice | solution.py:74
  135.1 7.8 %dynamic_update_slice.101 = bf16[1536,2432]{0,1:T(8,128)(2,1)} dynamic-update-slice(bf16[1536,2432]{0,1:T(8,128)(2,1)} %dynamic_update_slice.100, bf16[96,2432]{0,1:T(8,128)(2,1)S(1)} %copy.52, s32[]{:T(128)S(6)} %select_n.906, s32[]{:T(128)} %constant.1034.clone.1) | dynamic-update-slice | bytes 933892 | tf_op jit(solution)/shard_map/dynamic_update_slice | solution.py:74
  144.3 7.8 %dynamic_update_slice.102 = bf16[1536,2432]{0,1:T(8,128)(2,1)} dynamic-update-slice(bf16[1536,2432]{0,1:T(8,128)(2,1)} %dynamic_update_slice.101, bf16[96,2432]{0,1:T(8,128)(2,1)S(1)} %copy.53, s32[]{:T(128)S(6)} %select_n.910, s32[]{:T(128)} %constant.1034.clone.1) | dynamic-update-slice | bytes 933892 | tf_op jit(solution)/shard_map/dynamic_update_slice | solution.py:74
  166.7 7.8 %dynamic_update_slice.103 = bf16[1536,2432]{0,1:T(8,128)(2,1)} dynamic-update-slice(bf16[1536,2432]{0,1:T(8,128)(2,1)} %dynamic_update_slice.102, bf16[96,2432]{0,1:T(8,128)(2,1)S(1)} %copy.54, s32[]{:T(128)S(6)} %select_n.914, s32[]{:T(128)} %constant.1034.clone.1) | dynamic-update-slice | bytes 933892 | tf_op jit(solution)/shard_map/dynamic_update_slice | solution.py:74
  175.8 7.8 %dynamic_update_slice.104 = bf16[1536,2432]{0,1:T(8,128)(2,1)} dynamic-update-slice(bf16[1536,2432]{0,1:T(8,128)(2,1)} %dynamic_update_slice.103, bf16[96,2432]{0,1:T(8,128)(2,1)S(1)} %copy.55, s32[]{:T(128)S(6)} %select_n.918, s32[]{:T(128)} %constant.1034.clone.1) | dynamic-update-slice | bytes 933892 | tf_op jit(solution)/shard_map/dynamic_update_slice | solution.py:74
  216.5 7.8 %dynamic_update_slice.107 = bf16[1536,2432]{0,1:T(8,128)(2,1)} dynamic-update-slice(bf16[1536,2432]{0,1:T(8,128)(2,1)} %dynamic_update_slice.106, bf16[96,2432]{0,1:T(8,128)(2,1)S(1)} %copy.58, s32[]{:T(128)S(6)} %select_n.930, s32[]{:T(128)} %constant.1034.clone.1) | dynamic-update-slice | bytes 933892 | tf_op jit(solution)/shard_map/dynamic_update_slice | solution.py:74
  233.9 7.8 %dynamic_update_slice.109 = bf16[1536,2432]{0,1:T(8,128)(2,1)} dynamic-update-slice(bf16[1536,2432]{0,1:T(8,128)(2,1)} %dynamic_update_slice.108, bf16[96,2432]{0,1:T(8,128)(2,1)S(1)} %copy.60, s32[]{:T(128)S(6)} %select_n.938, s32[]{:T(128)} %constant.1034.clone.1) | dynamic-update-slice | bytes 933892 | tf_op jit(solution)/shard_map/dynamic_update_slice | solution.py:74
  254.6 7.8 %dynamic_update_slice.111 = bf16[1536,2432]{0,1:T(8,128)(2,1)} dynamic-update-slice(bf16[1536,2432]{0,1:T(8,128)(2,1)} %dynamic_update_slice.110, bf16[96,2432]{0,1:T(8,128)(2,1)S(1)} %copy.62, s32[]{:T(128)S(6)} %select_n.946, s32[]{:T(128)} %constant.1034.clone.1) | dynamic-update-slice | bytes 933892 | tf_op jit(solution)/shard_map/dynamic_update_slice | solution.py:74
  263.2 10.4 %fusion.23.q_in.k_in.v_in = f32[1536,1024]{1,0:T(8,128)} fusion(bf16[1536,2432]{0,1:T(8,128)(2,1)} %dynamic_update_slice.111, f32[1536]{0:T(1024)S(1)} %get-tuple-element.28, f32[1024]{0:T(1024)S(1)} %add_rsqrt_fusion, bf16[512,1536]{1,0:T(8,128)(2,1)} %collective-permute-done.15, bf16[512,1536]{1,0:T(8,128)(2,1)S(1)} %bitcast.277), kind=kOutput, calls=%fused_computation.35 | convolution fusion | flops 4842848256 | bytes 14166016 | tf_op jit(solution)/shard_map/dot_general | solution.py:27
  273.6 14.9 %attend.1 = (bf16[768,1024]{1,0:T(8,128)(2,1)S(1)}, bf16[768,1024]{1,0:T(8,128)(2,1)S(1)}, bf16[384,1024]{1,0:T(8,128)(2,1)S(1)}, bf16[384,1024]{1,0:T(8,128)(2,1)S(1)}, f32[4,2,1024]{2,1,0:T(2,128)S(1)}) custom-call(s32[1]{0:T(128)} %bitcast.1.side_ref, f32[1536,1024]{1,0:T(8,128)} %fusion.23.q_in.k_in.v_in, f32[1536,1024]{1,0:T(8,128)} %fusion.23.q_in.k_in.v_in, ...), custom_call_target="tpu_custom_call" | custom-call | flops 3221225472 | bytes 12582912 | tf_op jit(solution)/shard_map/attend/pallas_call | solution.py:188
  301.7 22.3 %collective-permute-done.16 = bf16[512,1536]{1,0:T(8,128)(2,1)S(1)} collective-permute-done((bf16[512,1536]{1,0:T(8,128)(2,1)S(1)}, bf16[512,1536]{1,0:T(8,128)(2,1)S(1)}, u32[]{:S(2)}, u32[]{:S(2)}) %collective-permute-start.16) | collective-permute-done | bytes 1572896 | tf_op jit(solution)/shard_map/ppermute | solution.py:33
  331.9 12.3 %collective-permute-done.29 = bf16[96,6144]{1,0:T(8,128)(2,1)S(1)} collective-permute-done((bf16[96,6144]{1,0:T(8,128)(2,1)S(1)}, bf16[96,6144]{1,0:T(8,128)(2,1)S(1)}, u32[]{:S(2)}, u32[]{:S(2)}) %collective-permute-start.29) | collective-permute-done | bytes 1179680 | tf_op jit(solution)/shard_map/ppermute | solution.py:79
  348.9 11.7 %collective-permute-done.31 = bf16[96,6144]{1,0:T(8,128)(2,1)S(1)} collective-permute-done((bf16[96,6144]{1,0:T(8,128)(2,1)S(1)}, bf16[96,6144]{1,0:T(8,128)(2,1)S(1)}, u32[]{:S(2)}, u32[]{:S(2)}) %collective-permute-start.31) | collective-permute-done | bytes 1179680 | tf_op jit(solution)/shard_map/ppermute | solution.py:79
  364.5 11.5 %fusion.11 = f32[1024,2048]{1,0:T(8,128)} fusion(bf16[1536,6144]{1,0:T(8,128)(2,1)} %constant_dynamic-update-slice_fusion.1, bf16[512,1536]{1,0:T(8,128)(2,1)S(1)} %collective-permute-done.17, bf16[512,1536]{1,0:T(8,128)(2,1)S(1)} %multiply_convert_fusion.4), kind=kOutput, calls=%fused_computation.22 | convolution fusion | flops 6448742400 | bytes 17825792 | tf_op jit(solution)/shard_map/dot_general | solution.py:27
  376.0 11.8 %fusion.1 = f32[1024,2048]{1,0:T(8,128)} fusion(bf16[1536,6144]{1,0:T(8,128)(2,1)} %constant_dynamic-update-slice_fusion.1, bf16[512,1536]{1,0:T(8,128)(2,1)} %collective-permute-done.34, bf16[512,1536]{1,0:T(8,128)(2,1)} %bitcast.25), kind=kOutput, calls=%fused_computation.12 | convolution fusion | flops 6448742400 | bytes 17825792 | tf_op jit(solution)/shard_map/dot_general | solution.py:27
  387.8 17.6 %multiply_convert_fusion.1 = (bf16[1024,2048]{1,0:T(8,128)(2,1)}, bf16[1024,2048]{1,0:T(8,128)(2,1)}, bf16[1024,2048]{1,0:T(8,128)(2,1)}) fusion(f32[1024,2048]{1,0:T(8,128)} %fusion.1, f32[1024,2048]{1,0:T(8,128)} %fusion.11, bf16[1536,6144]{1,0:T(8,128)(2,1)} %constant_dynamic-update-slice_fusion.1, bf16[512,1536]{1,0:T(8,128)(2,1)} %copy-done.34, ...), kind=kOutput, calls=%fused_computation.1 | convolution fusion | flops 6480199680 | bytes 38797312 | tf_op jit(solution)/shard_map/dot_general | solution.py:27
  405.4 9.7 %convolution_convert_fusion.1 = bf16[1536,2048]{1,0:T(8,128)(2,1)S(1)} fusion(bf16[1024,2048]{1,0:T(8,128)(2,1)} %get-tuple-element.38, bf16[512,1536]{1,0:T(8,128)(2,1)} %collective-permute-done.34, bf16[512,1536]{1,0:T(8,128)(2,1)} %bitcast.25), kind=kOutput, calls=%fused_computation.6 | convolution fusion | flops 6451888128 | bytes 13631488 | tf_op jit(solution)/shard_map/dot_general | solution.py:27
  426.4 7.4 convolution_convert_fusion.2
  439.0 7.4 convolution_convert_fusion.3
  472.3 21.4 %collective-permute-done.35 = bf16[512,1536]{1,0:T(8,128)(2,1)S(1)} collective-permute-done((bf16[512,1536]{1,0:T(8,128)(2,1)S(1)}, bf16[512,1536]{1,0:T(8,128)(2,1)S(1)}, u32[]{:S(2)}, u32[]{:S(2)}) %collective-permute-start.35) | collective-permute-done | bytes 1572896 | tf_op jit(solution)/shard_map/ppermute | solution.py:33
  504.4 23.1 %collective-permute-done.33 = bf16[512,1536]{1,0:T(8,128)(2,1)S(1)} collective-permute-done((bf16[512,1536]{1,0:T(8,128)(2,1)}, bf16[512,1536]{1,0:T(8,128)(2,1)S(1)}, u32[]{:S(2)}, u32[]{:S(2)}) %collective-permute-start.33) | collective-permute-done | bytes 1572896 | tf_op jit(solution)/shard_map/ppermute | solution.py:33
  527.5 8.1 %fusion.52 = bf16[1,512,1536]{2,1,0:T(8,128)(2,1)} fusion(f32[512,1536]{1,0:T(8,128)S(1)} %copy-done.4, bf16[512,1536]{1,0:T(8,128)(2,1)S(1)} %collective-permute-done.33, bf16[1536,6144]{1,0:T(8,128)(2,1)} %constant_dynamic-update-slice_fusion.1, bf16[1024,2048]{1,0:T(8,128)(2,1)} %get-tuple-element.38), kind=kOutput, calls=%fused_computation.69 | convolution fusion | flops 3224371200 | bytes 14680064 | tf_op jit(solution)/shard_map/dot_general | solution.py:27
  546.4 14.4 %collective-permute-done.36 = bf16[512,1536]{1,0:T(8,128)(2,1)S(1)} collective-permute-done((bf16[512,1536]{1,0:T(8,128)(2,1)S(1)}, bf16[512,1536]{1,0:T(8,128)(2,1)S(1)}, u32[]{:S(2)}, u32[]{:S(2)}) %collective-permute-start.36) | collective-permute-done | bytes 1572896 | tf_op jit(solution)/shard_map/ppermute | solution.py:33
  565.7 20.2 %attend_back.1 = (bf16[768,1024]{1,0:T(8,128)(2,1)S(1)}, bf16[384,1024]{1,0:T(8,128)(2,1)S(1)}, bf16[384,1024]{1,0:T(8,128)(2,1)S(1)}) custom-call(s32[1]{0:T(128)} %bitcast.1.side_ref, bf16[768,1024]{1,0:T(8,128)(2,1)} %copy-done.2, bf16[384,1024]{1,0:T(8,128)(2,1)S(1)} %get-tuple-element.21.k_ref, bf16[384,1024]{1,0:T(8,128)(2,1)S(1)} %get-tuple-element.22.v_ref, ...), custom_call_target="tpu_custom_call" | custom-call | flops 8053063680 | bytes 12582912 | tf_op jit(solution)/shard_map/attend_back/pallas_call | solution.py:312
  591.1 9.3 %convolution_convert_fusion = bf16[1536,1536]{0,1:T(8,128)(2,1)} fusion(bf16[1536,1024]{1,0:T(8,128)(2,1)S(1)} %constant_dynamic-update-slice_fusion.16, f32[1536]{0:T(1024)S(1)} %copy-done.27, f32[1024]{0:T(1024)S(1)} %copy-done.29, bf16[512,1536]{1,0:T(8,128)(2,1)} %collective-permute-done.15, bf16[512,1536]{1,0:T(8,128)(2,1)S(1)} %bitcast.278), kind=kOutput, calls=%fused_computation.5 | convolution fusion | flops 4845207552 | bytes 11020288 | tf_op jit(solution)/shard_map/dot_general | solution.py:27
  635.3 7.3 fusion.41
  648.7 10.1 %copy.63 = bf16[1536,2432]{1,0:T(8,128)(2,1)} copy(bf16[1536,2432]{0,1:T(8,128)(2,1)} %pad_maximum_fusion) | data formatting | bytes 14942208 | tf_op jit(solution)/shard_map/concatenate | solution.py:456
  687.6 10.4 %collective-permute-done.39 = bf16[96,2432]{1,0:T(8,128)(2,1)S(1)} collective-permute-done((bf16[96,2432]{1,0:T(8,128)(2,1)S(1)}, bf16[96,2432]{1,0:T(8,128)(2,1)S(1)}, u32[]{:S(2)}, u32[]{:S(2)}) %collective-permute-start.39) | collective-permute-done | bytes 466976 | tf_op jit(solution)/shard_map/ppermute | solution.py:106
  (365 shorter events, 358.5 us)
Async XLA Ops:
  26.2 99.0 %collective-permute-start.18 = (bf16[96,6144]{1,0:T(8,128)(2,1)}, bf16[96,6144]{1,0:T(8,128)(2,1)}, u32[]{:S(2)}, u32[]{:S(2)}) collective-permute-start(bf16[96,6144]{1,0:T(8,128)(2,1)} %get-tuple-element.39), channel_id=1, source_target_pairs={{0,2},{2,0},{4,6},{6,4},{8,10},{10,8},{12,14},{14,12},{16,18},{18,... | collective-permute-start | bytes 3538952 | tf_op jit(solution)/shard_map/ppermute | solution.py:80
  26.6 96.9 %collective-permute-start.19 = (bf16[96,6144]{1,0:T(8,128)(2,1)}, bf16[96,6144]{1,0:T(8,128)(2,1)}, u32[]{:S(2)}, u32[]{:S(2)}) collective-permute-start(bf16[96,6144]{1,0:T(8,128)(2,1)} %get-tuple-element.39), channel_id=1, source_target_pairs={{0,8},{10,2},{8,16},{18,10},{16,24},{26,18},{24,28},{30,26},{28,20... | collective-permute-start | bytes 3538952 | tf_op jit(solution)/shard_map/ppermute | solution.py:79
  29.5 55.3 %collective-permute-start = (bf16[96,2432]{1,0:T(8,128)(2,1)S(1)}, bf16[96,2432]{1,0:T(8,128)(2,1)}, u32[]{:S(2)}, u32[]{:S(2)}) collective-permute-start(bf16[96,2432]{1,0:T(8,128)(2,1)S(1)} %pad_dynamic-update-slice_fusion), channel_id=1, source_target_pairs={{0,2},{2,0},{4,6},{6,4},{8,10},{10,8},{12,14},{14,12},{16,18},{18,... | collective-permute-start | bytes 1400840 | tf_op jit(solution)/shard_map/ppermute | solution.py:80
  48.6 56.2 %collective-permute-start.2 = (bf16[96,2432]{1,0:T(8,128)(2,1)}, bf16[96,2432]{1,0:T(8,128)(2,1)}, u32[]{:S(2)}, u32[]{:S(2)}) collective-permute-start(bf16[96,2432]{1,0:T(8,128)(2,1)} %collective-permute-done.1), channel_id=1, source_target_pairs={{0,2},{2,0},{4,6},{6,4},{8,10},{10,8},{12,14},{14,12},{16,18},{18,... | collective-permute-start | bytes 1400840 | tf_op jit(solution)/shard_map/ppermute | solution.py:80
  49.2 64.7 %collective-permute-start.3 = (bf16[96,2432]{1,0:T(8,128)(2,1)}, bf16[96,2432]{1,0:T(8,128)(2,1)}, u32[]{:S(2)}, u32[]{:S(2)}) collective-permute-start(bf16[96,2432]{1,0:T(8,128)(2,1)} %collective-permute-done.1), channel_id=1, source_target_pairs={{0,8},{10,2},{8,16},{18,10},{16,24},{26,18},{24,28},{30,26},{28,20... | collective-permute-start | bytes 1400840 | tf_op jit(solution)/shard_map/ppermute | solution.py:79
  84.8 68.1 %collective-permute-start.15 = (bf16[512,1536]{1,0:T(8,128)(2,1)S(1)}, bf16[512,1536]{1,0:T(8,128)(2,1)}, u32[]{:S(2)}, u32[]{:S(2)}) collective-permute-start(bf16[512,1536]{1,0:T(8,128)(2,1)S(1)} %bitcast.273), channel_id=1, source_target_pairs={{0,1},{1,0},{2,3},{3,2},{4,5},{5,4},{6,7},{7,6},{8,9},{9,8},{10,11... | collective-permute-start | bytes 4718600 | tf_op jit(solution)/shard_map/ppermute | solution.py:33
  123.6 80.2 %collective-permute-start.20 = (bf16[96,6144]{1,0:T(8,128)(2,1)}, bf16[96,6144]{1,0:T(8,128)(2,1)}, u32[]{:S(2)}, u32[]{:S(2)}) collective-permute-start(bf16[96,6144]{1,0:T(8,128)(2,1)} %collective-permute-done.19), channel_id=1, source_target_pairs={{0,2},{2,0},{4,6},{6,4},{8,10},{10,8},{12,14},{14,12},{16,18},{18,... | collective-permute-start | bytes 3538952 | tf_op jit(solution)/shard_map/ppermute | solution.py:80
  125.2 77.6 %collective-permute-start.21 = (bf16[96,6144]{1,0:T(8,128)(2,1)}, bf16[96,6144]{1,0:T(8,128)(2,1)}, u32[]{:S(2)}, u32[]{:S(2)}) collective-permute-start(bf16[96,6144]{1,0:T(8,128)(2,1)} %collective-permute-done.19), channel_id=1, source_target_pairs={{0,8},{10,2},{8,16},{18,10},{16,24},{26,18},{24,28},{30,26},{28,20... | collective-permute-start | bytes 3538952 | tf_op jit(solution)/shard_map/ppermute | solution.py:79
  155.1 36.9 %collective-permute-start.9 = (bf16[96,2432]{1,0:T(8,128)(2,1)}, bf16[96,2432]{1,0:T(8,128)(2,1)S(1)}, u32[]{:S(2)}, u32[]{:S(2)}) collective-permute-start(bf16[96,2432]{1,0:T(8,128)(2,1)} %collective-permute-done.7), channel_id=1, source_target_pairs={{0,8},{10,2},{8,16},{18,10},{16,24},{26,18},{24,28},{30,26},{28,20... | collective-permute-start | bytes 1400840 | tf_op jit(solution)/shard_map/ppermute | solution.py:79
  202.8 49.0 %collective-permute-start.22 = (bf16[96,6144]{1,0:T(8,128)(2,1)}, bf16[96,6144]{1,0:T(8,128)(2,1)}, u32[]{:S(2)}, u32[]{:S(2)}) collective-permute-start(bf16[96,6144]{1,0:T(8,128)(2,1)} %collective-permute-done.21), channel_id=1, source_target_pairs={{0,2},{2,0},{4,6},{6,4},{8,10},{10,8},{12,14},{14,12},{16,18},{18,... | collective-permute-start | bytes 3538952 | tf_op jit(solution)/shard_map/ppermute | solution.py:80
  202.8 47.0 %collective-permute-start.23 = (bf16[96,6144]{1,0:T(8,128)(2,1)}, bf16[96,6144]{1,0:T(8,128)(2,1)}, u32[]{:S(2)}, u32[]{:S(2)}) collective-permute-start(bf16[96,6144]{1,0:T(8,128)(2,1)} %collective-permute-done.21), channel_id=1, source_target_pairs={{0,8},{10,2},{8,16},{18,10},{16,24},{26,18},{24,28},{30,26},{28,20... | collective-permute-start | bytes 3538952 | tf_op jit(solution)/shard_map/ppermute | solution.py:79
  214.7 161.3 %collective-permute-start.34 = (bf16[512,1536]{1,0:T(8,128)(2,1)}, bf16[512,1536]{1,0:T(8,128)(2,1)}, u32[]{:S(2)}, u32[]{:S(2)}) collective-permute-start(bf16[512,1536]{1,0:T(8,128)(2,1)} %bitcast.25), channel_id=1, source_target_pairs={{0,1},{1,0},{2,3},{3,2},{4,5},{5,4},{6,7},{7,6},{8,9},{9,8},{10,11... | collective-permute-start | bytes 4718600 | tf_op jit(solution)/shard_map/ppermute | solution.py:33
  249.8 47.2 %collective-permute-start.24 = (bf16[96,6144]{1,0:T(8,128)(2,1)}, bf16[96,6144]{1,0:T(8,128)(2,1)}, u32[]{:S(2)}, u32[]{:S(2)}) collective-permute-start(bf16[96,6144]{1,0:T(8,128)(2,1)} %collective-permute-done.23), channel_id=1, source_target_pairs={{0,2},{2,0},{4,6},{6,4},{8,10},{10,8},{12,14},{14,12},{16,18},{18,... | collective-permute-start | bytes 3538952 | tf_op jit(solution)/shard_map/ppermute | solution.py:80
  250.3 43.6 %collective-permute-start.25 = (bf16[96,6144]{1,0:T(8,128)(2,1)}, bf16[96,6144]{1,0:T(8,128)(2,1)}, u32[]{:S(2)}, u32[]{:S(2)}) collective-permute-start(bf16[96,6144]{1,0:T(8,128)(2,1)} %collective-permute-done.23), channel_id=1, source_target_pairs={{0,8},{10,2},{8,16},{18,10},{16,24},{26,18},{24,28},{30,26},{28,20... | collective-permute-start | bytes 3538952 | tf_op jit(solution)/shard_map/ppermute | solution.py:79
  290.0 34.1 %collective-permute-start.16 = (bf16[512,1536]{1,0:T(8,128)(2,1)S(1)}, bf16[512,1536]{1,0:T(8,128)(2,1)S(1)}, u32[]{:S(2)}, u32[]{:S(2)}) collective-permute-start(bf16[512,1536]{1,0:T(8,128)(2,1)S(1)} %convolution_convert_fusion.5), channel_id=1, source_target_pairs={{0,1},{1,0},{2,3},{3,2},{4,5},{5,4},{6,7},{7,6},{8,9},{9,8},{10,11... | collective-permute-start | bytes 4718600 | tf_op jit(solution)/shard_map/ppermute | solution.py:33
  293.9 35.7 %collective-permute-start.26 = (bf16[96,6144]{1,0:T(8,128)(2,1)}, bf16[96,6144]{1,0:T(8,128)(2,1)S(1)}, u32[]{:S(2)}, u32[]{:S(2)}) collective-permute-start(bf16[96,6144]{1,0:T(8,128)(2,1)} %collective-permute-done.25), channel_id=1, source_target_pairs={{0,2},{2,0},{4,6},{6,4},{8,10},{10,8},{12,14},{14,12},{16,18},{18,... | collective-permute-start | bytes 3538952 | tf_op jit(solution)/shard_map/ppermute | solution.py:80
  293.9 34.0 %collective-permute-start.27 = (bf16[96,6144]{1,0:T(8,128)(2,1)}, bf16[96,6144]{1,0:T(8,128)(2,1)S(1)}, u32[]{:S(2)}, u32[]{:S(2)}) collective-permute-start(bf16[96,6144]{1,0:T(8,128)(2,1)} %collective-permute-done.25), channel_id=1, source_target_pairs={{0,8},{10,2},{8,16},{18,10},{16,24},{26,18},{24,28},{30,26},{28,20... | collective-permute-start | bytes 3538952 | tf_op jit(solution)/shard_map/ppermute | solution.py:79
  326.3 38.2 %collective-permute-start.17 = (bf16[512,1536]{1,0:T(8,128)(2,1)S(1)}, bf16[512,1536]{1,0:T(8,128)(2,1)S(1)}, u32[]{:S(2)}, u32[]{:S(2)}) collective-permute-start(bf16[512,1536]{1,0:T(8,128)(2,1)S(1)} %multiply_convert_fusion.4), channel_id=1, source_target_pairs={{0,1},{1,0},{2,3},{3,2},{4,5},{5,4},{6,7},{7,6},{8,9},{9,8},{10,11... | collective-permute-start | bytes 4718600 | tf_op jit(solution)/shard_map/ppermute | solution.py:33
  419.6 115.9 %collective-permute-start.63 = (bf16[8,96,2048]{2,1,0:T(8,128)(2,1)}, bf16[8,96,2048]{2,1,0:T(8,128)(2,1)}, u32[]{:S(2)}, u32[]{:S(2)}) collective-permute-start(bf16[8,96,2048]{2,1,0:T(8,128)(2,1)} %dynamic-slice_bitcast_fusion.1), channel_id=1, source_target_pairs={{0,2},{2,0},{4,6},{6,4},{8,10},{10,8},{12,14},{14,12},{16,18},{18,... | collective-permute-start | bytes 9437192 | tf_op jit(solution)/shard_map/ppermute | solution.py:97
  438.3 100.9 %collective-permute-start.55 = (bf16[8,96,2048]{2,1,0:T(8,128)(2,1)}, bf16[8,96,2048]{2,1,0:T(8,128)(2,1)}, u32[]{:S(2)}, u32[]{:S(2)}) collective-permute-start(bf16[8,96,2048]{2,1,0:T(8,128)(2,1)} %dynamic-slice_bitcast_fusion.2), channel_id=1, source_target_pairs={{0,2},{2,0},{4,6},{6,4},{8,10},{10,8},{12,14},{14,12},{16,18},{18,... | collective-permute-start | bytes 9437192 | tf_op jit(solution)/shard_map/ppermute | solution.py:97
  450.0 93.0 %collective-permute-start.47 = (bf16[8,96,2048]{2,1,0:T(8,128)(2,1)}, bf16[8,96,2048]{2,1,0:T(8,128)(2,1)}, u32[]{:S(2)}, u32[]{:S(2)}) collective-permute-start(bf16[8,96,2048]{2,1,0:T(8,128)(2,1)} %dynamic-slice_bitcast_fusion.3), channel_id=1, source_target_pairs={{0,2},{2,0},{4,6},{6,4},{8,10},{10,8},{12,14},{14,12},{16,18},{18,... | collective-permute-start | bytes 9437192 | tf_op jit(solution)/shard_map/ppermute | solution.py:97
  456.5 37.3 %collective-permute-start.35 = (bf16[512,1536]{1,0:T(8,128)(2,1)S(1)}, bf16[512,1536]{1,0:T(8,128)(2,1)S(1)}, u32[]{:S(2)}, u32[]{:S(2)}) collective-permute-start(bf16[512,1536]{1,0:T(8,128)(2,1)S(1)} %fusion.49), channel_id=1, source_target_pairs={{0,1},{1,0},{2,3},{3,2},{4,5},{5,4},{6,7},{7,6},{8,9},{9,8},{10,11... | collective-permute-start | bytes 4718600 | tf_op jit(solution)/shard_map/ppermute | solution.py:33
  464.4 63.1 %collective-permute-start.33 = (bf16[512,1536]{1,0:T(8,128)(2,1)}, bf16[512,1536]{1,0:T(8,128)(2,1)S(1)}, u32[]{:S(2)}, u32[]{:S(2)}) collective-permute-start(bf16[512,1536]{1,0:T(8,128)(2,1)} %fusion.43), channel_id=1, source_target_pairs={{0,1},{1,0},{2,3},{3,2},{4,5},{5,4},{6,7},{7,6},{8,9},{9,8},{10,11... | collective-permute-start | bytes 4718600 | tf_op jit(solution)/shard_map/ppermute | solution.py:33
  503.8 57.0 %collective-permute-start.36 = (bf16[512,1536]{1,0:T(8,128)(2,1)S(1)}, bf16[512,1536]{1,0:T(8,128)(2,1)S(1)}, u32[]{:S(2)}, u32[]{:S(2)}) collective-permute-start(bf16[512,1536]{1,0:T(8,128)(2,1)S(1)} %fusion.140), channel_id=1, source_target_pairs={{0,1},{1,0},{2,3},{3,2},{4,5},{5,4},{6,7},{7,6},{8,9},{9,8},{10,11... | collective-permute-start | bytes 4718600 | tf_op jit(solution)/shard_map/ppermute | solution.py:33
  536.7 67.9 %collective-permute-start.64 = (bf16[96,2048]{1,0:T(8,128)(2,1)S(1)}, bf16[96,2048]{1,0:T(8,128)(2,1)}, u32[]{:S(2)}, u32[]{:S(2)}) collective-permute-start(bf16[96,2048]{1,0:T(8,128)(2,1)S(1)} %fusion.101), channel_id=1, source_target_pairs={{0,8},{10,2},{8,16},{18,10},{16,24},{26,18},{24,28},{30,26},{28,20... | collective-permute-start | bytes 1179656 | tf_op jit(solution)/shard_map/ppermute | solution.py:106
  540.5 68.0 %collective-permute-start.56 = (bf16[96,2048]{1,0:T(8,128)(2,1)S(1)}, bf16[96,2048]{1,0:T(8,128)(2,1)}, u32[]{:S(2)}, u32[]{:S(2)}) collective-permute-start(bf16[96,2048]{1,0:T(8,128)(2,1)S(1)} %fusion.115), channel_id=1, source_target_pairs={{0,8},{10,2},{8,16},{18,10},{16,24},{26,18},{24,28},{30,26},{28,20... | collective-permute-start | bytes 1179656 | tf_op jit(solution)/shard_map/ppermute | solution.py:106
  544.2 68.3 %collective-permute-start.48 = (bf16[96,2048]{1,0:T(8,128)(2,1)S(1)}, bf16[96,2048]{1,0:T(8,128)(2,1)}, u32[]{:S(2)}, u32[]{:S(2)}) collective-permute-start(bf16[96,2048]{1,0:T(8,128)(2,1)S(1)} %fusion.129), channel_id=1, source_target_pairs={{0,8},{10,2},{8,16},{18,10},{16,24},{26,18},{24,28},{30,26},{28,20... | collective-permute-start | bytes 1179656 | tf_op jit(solution)/shard_map/ppermute | solution.py:106
  590.6 44.7 %collective-permute-start.37 = (bf16[512,1536]{1,0:T(8,128)(2,1)S(1)}, bf16[512,1536]{1,0:T(8,128)(2,1)S(1)}, u32[]{:S(2)}, u32[]{:S(2)}) collective-permute-start(bf16[512,1536]{1,0:T(8,128)(2,1)S(1)} %get-tuple-element.68), channel_id=1, source_target_pairs={{0,1},{1,0},{2,3},{3,2},{4,5},{5,4},{6,7},{7,6},{8,9},{9,8},{10,11... | collective-permute-start | bytes 4718600 | tf_op jit(solution)/shard_map/ppermute | solution.py:33
  623.6 37.9 %collective-permute-start.50 = (bf16[96,2048]{1,0:T(8,128)(2,1)S(1)}, bf16[96,2048]{1,0:T(8,128)(2,1)S(1)}, u32[]{:S(2)}, u32[]{:S(2)}) collective-permute-start(bf16[96,2048]{1,0:T(8,128)(2,1)S(1)} %fusion.126), channel_id=1, source_target_pairs={{0,8},{10,2},{8,16},{18,10},{16,24},{26,18},{24,28},{30,26},{28,20... | collective-permute-start | bytes 1179656 | tf_op jit(solution)/shard_map/ppermute | solution.py:106
  627.8 37.6 %collective-permute-start.67 = (bf16[96,2048]{1,0:T(8,128)(2,1)S(1)}, bf16[96,2048]{1,0:T(8,128)(2,1)}, u32[]{:S(2)}, u32[]{:S(2)}) collective-permute-start(bf16[96,2048]{1,0:T(8,128)(2,1)S(1)} %fusion.96), channel_id=1, source_target_pairs={{0,8},{10,2},{8,16},{18,10},{16,24},{26,18},{24,28},{30,26},{28,20... | collective-permute-start | bytes 1179656 | tf_op jit(solution)/shard_map/ppermute | solution.py:106
  632.7 36.2 %collective-permute-start.59 = (bf16[96,2048]{1,0:T(8,128)(2,1)}, bf16[96,2048]{1,0:T(8,128)(2,1)}, u32[]{:S(2)}, u32[]{:S(2)}) collective-permute-start(bf16[96,2048]{1,0:T(8,128)(2,1)} %fusion.110), channel_id=1, source_target_pairs={{0,8},{10,2},{8,16},{18,10},{16,24},{26,18},{24,28},{30,26},{28,20... | collective-permute-start | bytes 1179656 | tf_op jit(solution)/shard_map/ppermute | solution.py:106
  687.0 31.8 %collective-permute-start.53 = (bf16[96,2048]{1,0:T(8,128)(2,1)S(1)}, bf16[96,2048]{1,0:T(8,128)(2,1)S(1)}, u32[]{:S(2)}, u32[]{:S(2)}) collective-permute-start(bf16[96,2048]{1,0:T(8,128)(2,1)S(1)} %fusion.120), channel_id=1, source_target_pairs={{0,8},{10,2},{8,16},{18,10},{16,24},{26,18},{24,28},{30,26},{28,20... | collective-permute-start | bytes 1179656 | tf_op jit(solution)/shard_map/ppermute | solution.py:106
  (88 other events, 1407.6 us)
